TPU v7x, 32 devices: a whole 2x2x4 slice. The times are simulated.
32 devices in a mesh: ctx: 8 (over z, y), ep: 4 (over x, core).
Axes of the slice: x: 2, y: 2, z: 4, core: 2. Of those that a mesh axis runs over, the one named last changes fastest.
Arguments:
- tokens: bfloat16 [12288, 2048], P(('ctx', 'ep')), may hold values from -6 to 6
- expert_ids: int32 [12288, 8], P(('ctx', 'ep')), may hold values from 0 to 127, as said below
- gate_codes: int32 [12288, 8], P(('ctx', 'ep')), may hold values from 4096 to 65536
- out_grad: bfloat16 [12288, 2048], P(('ctx', 'ep')), may hold values from -6 to 6
- expert_weights: bfloat16 [2048, 4, 3, 768], P('ctx', 'ep'), may hold values from -0.21875 to 0.21875
Outputs:
- moe_out: bfloat16 [12288, 2048], P(('ctx', 'ep'))
- input_grad: bfloat16 [12288, 2048], P(('ctx', 'ep'))
- weight_grads: float32 [2048, 4, 3, 768], P('ctx', 'ep')
Inputs may be any that keep to these rules, and one draw needn't show every extreme that they name: `expert_ids`: each row names 8 different experts. Within each aligned block of 384 rows (the rows of one device), every expert below 4 is named by 1 to 24 rows, and one expert below 4, the same in every block, is named by exactly 24 rows in every block.
All inputs are finite; a program needn't handle non-finite values.
Results may differ from a plain program's by a relative error of at most 0.015.
Values may be sent and summed in bfloat16 or wider, within the bound.
No kernel may reach another device: no remote copies, remote signals or barrier semaphores. Data moves between devices by JAX's collectives and lax.ppermute only.
A program may use at most 128 MiB of HBM per device.

v0:
```python
import jax
import jax.numpy as jnp
from jax import lax
from jax.sharding import PartitionSpec as P

EXP_DEV = 1
CAP = 24


def body(tokens, expert_ids, gate_codes, out_grad, expert_weights):
    n_owner = lax.axis_size("ep")
    wave_size = n_owner * EXP_DEV
    width = tokens.shape[1]
    gates = gate_codes.astype(jnp.float32) / 65536.0
    wave_range = jnp.arange(wave_size, dtype=jnp.int32)
    chosen = expert_ids[:, :, None] == wave_range[None, None, :]
    member = jnp.any(chosen, axis=1)
    route_weight = jnp.sum(jnp.where(chosen, gates[:, :, None], 0.0), axis=1)
    position = jnp.cumsum(member.astype(jnp.int32), axis=0) - 1
    placed = member[:, :, None] & (
        position[:, :, None] == jnp.arange(CAP, dtype=jnp.int32)[None, None, :]
    )
    onehot = placed.astype(jnp.bfloat16)
    slot_rows = jnp.einsum(
        "tec,td->ecd", onehot, tokens, preferred_element_type=jnp.float32
    ).astype(jnp.bfloat16)
    slot_cotan = jnp.einsum("tec,td->ecd", onehot, out_grad, preferred_element_type=jnp.float32)
    slot_weight = jnp.sum(jnp.where(placed, route_weight[:, :, None], 0.0), axis=0)
    slot_grad = (slot_weight[:, :, None] * slot_cotan).astype(jnp.bfloat16)
    send_rows = slot_rows.reshape(n_owner, EXP_DEV, CAP, width)
    send_grad = slot_grad.reshape(n_owner, EXP_DEV, CAP, width)
    rows_in, grad_in = (
        lax.all_to_all(send_rows, "ep", split_axis=0, concat_axis=0, tiled=True),
        lax.all_to_all(send_grad, "ep", split_axis=0, concat_axis=0, tiled=True),
    )
    gathered = lax.all_gather(expert_weights, "ctx", axis=0, tiled=True)
    pre_gate = jnp.einsum(
        "sjcd,djf->sjcf", rows_in, gathered[:, :, 0, :], preferred_element_type=jnp.float32
    )
    pre_up = jnp.einsum(
        "sjcd,djf->sjcf", rows_in, gathered[:, :, 1, :], preferred_element_type=jnp.float32
    )
    soft = jax.nn.sigmoid(pre_gate)
    active = pre_gate * soft
    hidden = (active * pre_up).astype(jnp.bfloat16)
    expert_out = jnp.einsum(
        "sjcf,djf->sjcd", hidden, gathered[:, :, 2, :], preferred_element_type=jnp.float32
    ).astype(jnp.bfloat16)
    hidden_grad = jnp.einsum(
        "sjcd,djf->sjcf", grad_in, gathered[:, :, 2, :], preferred_element_type=jnp.float32
    )
    gate_grad = (hidden_grad * pre_up * soft * (1.0 + pre_gate * (1.0 - soft))).astype(jnp.bfloat16)
    up_grad = (hidden_grad * active).astype(jnp.bfloat16)
    route_input = (
        jnp.einsum(
            "sjcf,djf->sjcd", gate_grad, gathered[:, :, 0, :], preferred_element_type=jnp.float32
        )
        + jnp.einsum(
            "sjcf,djf->sjcd", up_grad, gathered[:, :, 1, :], preferred_element_type=jnp.float32
        )
    ).astype(jnp.bfloat16)
    out_back, input_back = (
        lax.all_to_all(expert_out, "ep", split_axis=0, concat_axis=0, tiled=True),
        lax.all_to_all(route_input, "ep", split_axis=0, concat_axis=0, tiled=True),
    )
    term_gate = jnp.einsum("sjcd,sjcf->djf", rows_in, gate_grad, preferred_element_type=jnp.float32)
    term_up = jnp.einsum("sjcd,sjcf->djf", rows_in, up_grad, preferred_element_type=jnp.float32)
    term_down = jnp.einsum("sjcd,sjcf->djf", grad_in, hidden, preferred_element_type=jnp.float32)
    full_terms = jnp.stack([term_gate, term_up, term_down], axis=2)
    weight_grads = lax.psum_scatter(
        full_terms.astype(jnp.bfloat16), "ctx", scatter_dimension=0, tiled=True
    ).astype(jnp.float32)
    out_back = out_back.reshape(wave_size, CAP, width)
    input_back = input_back.reshape(wave_size, CAP, width)
    combined = jnp.zeros((tokens.shape[0], width), jnp.float32)
    for expert in range(wave_size):
        picked = jnp.dot(onehot[:, expert, :], out_back[expert], preferred_element_type=jnp.float32)
        combined = combined + route_weight[:, expert : expert + 1] * picked
    input_grad = jnp.einsum("tec,ecd->td", onehot, input_back, preferred_element_type=jnp.float32)
    return (combined.astype(jnp.bfloat16), input_grad.astype(jnp.bfloat16), weight_grads)


def solution(mesh):
    placed = (
        P(("ctx", "ep"), None),
        P(("ctx", "ep"), None),
        P(("ctx", "ep"), None),
        P(("ctx", "ep"), None),
        P("ctx", "ep", None, None),
    )
    return jax.shard_map(
        body,
        mesh=mesh,
        in_specs=placed,
        out_specs=(P(("ctx", "ep"), None), P(("ctx", "ep"), None), P("ctx", "ep", None, None)),
        check_vma=False,
    )
```

profile of v0, /device:TPU:0, one launch (start us, length us, event | category | flops | bytes accessed | tf_op | source)
XLA Modules:
  0.0 339.1 jit_solution(9394798685926331807)
XLA Ops:
  7.2 0.7 all-gather.2.cloned.1.call-update
  7.9 0.9 fusion.38
  8.9 1.2 reduce-window.6
  10.6 0.7 convert_multiply_fusion
  11.3 0.7 select_reduce_fusion.1
  12.2 1.2 fusion.16
  13.3 4.2 %all-to-all-start.2 = ((bf16[4,1,24,2048]{3,2,1,0:T(8,128)(2,1)}), bf16[4,1,24,2048]{3,2,1,0:T(8,128)(2,1)S(1)}, u32[]{:S(2)}, u32[]{:S(2)}) async-start(bf16[4,1,24,2048]{3,2,1,0:T(8,128)(2,1)} %fusion.16), calls=%async_computation.2 | async-start | bytes 786432 | tf_op jit(solution)/shard_map/all_to_all | solution.py:34
  17.6 1.2 fusion.14
  18.7 6.2 %all-to-all-done.2 = bf16[4,1,24,2048]{3,2,1,0:T(8,128)(2,1)S(1)} async-done(((bf16[4,1,24,2048]{3,2,1,0:T(8,128)(2,1)}), bf16[4,1,24,2048]{3,2,1,0:T(8,128)(2,1)S(1)}, u32[]{:S(2)}, u32[]{:S(2)}) %all-to-all-start.2) | async-done | bytes 393248 | tf_op jit(solution)/shard_map/all_to_all | solution.py:34
  25.0 3.5 %all-to-all-start = ((bf16[4,1,24,2048]{3,2,1,0:T(8,128)(2,1)}), bf16[4,1,24,2048]{3,2,1,0:T(8,128)(2,1)S(1)}, u32[]{:S(2)}, u32[]{:S(2)}) async-start(bf16[4,1,24,2048]{3,2,1,0:T(8,128)(2,1)} %fusion.14), calls=%async_computation | async-start | bytes 786432 | tf_op jit(solution)/shard_map/all_to_all | solution.py:33
  28.5 121.7 %all-gather.2.cloned.1.call-done = bf16[2048,1,3,768]{3,0,2,1:T(8,128)(2,1)} async-done(((bf16[256,1,3,768]{3,0,2,1:T(8,128)(2,1)}), bf16[2048,1,3,768]{3,0,2,1:T(8,128)(2,1)}) %all-gather.2.cloned.1.call-update) | async-done | bytes 9437200 | tf_op jit(solution)/shard_map/all_gather | solution.py:36
  150.2 2.5 fusion.19
  152.7 2.5 fusion.20
  155.3 2.6 fusion.31
  157.9 1.0 fusion.2
  158.9 1.0 fusion.1
  159.9 1.0 fusion
  160.9 4.1 %pad_maximum_fusion = bf16[2048,1,3,768]{0,3,2,1:T(8,128)(2,1)} fusion(bf16[2048,1,1,768]{0,3,2,1:T(8,128)(2,1)S(1)} %fusion.2, bf16[2048,1,1,768]{0,3,2,1:T(8,128)(2,1)S(1)} %fusion.1, bf16[2048,1,1,768]{0,3,2,1:T(8,128)(2,1)S(1)} %fusion), kind=kLoop, calls=%fused_computation | loop fusion | flops 9437184 | bytes 18874368 | tf_op jit(solution)/shard_map/stack | solution.py:69
  165.1 3.0 fusion.3
  168.1 3.7 %fusion.15 = bf16[4,1,24,2048]{3,2,1,0:T(8,128)(2,1)} fusion(f32[4,24,2048]{2,1,0:T(8,128)S(1)} %fusion.3, bf16[4,24,768]{2,1,0:T(8,128)(2,1)S(1)} %get-tuple-element.19, bf16[2048,1,3,768]{3,0,2,1:T(8,128)(2,1)} %all-gather.2.cloned.1.call-done), kind=kOutput, calls=%fused_computation.26 | convolution fusion | flops 302383104 | bytes 4472832 | tf_op jit(solution)/shard_map/sjcf,djf->sjcd/dot_general | solution.py:58
  171.8 3.6 %all-to-all-start.3 = ((bf16[4,1,24,2048]{3,2,1,0:T(8,128)(2,1)}), bf16[4,1,24,2048]{3,2,1,0:T(8,128)(2,1)S(1)}, u32[]{:S(2)}, u32[]{:S(2)}) async-start(bf16[4,1,24,2048]{3,2,1,0:T(8,128)(2,1)} %fusion.15), calls=%async_computation.3 | async-start | bytes 786432 | tf_op jit(solution)/shard_map/all_to_all | solution.py:64
  175.4 3.7 %fusion.13 = bf16[4,1,24,2048]{3,2,1,0:T(8,128)(2,1)} fusion(bf16[4,24,768]{2,1,0:T(8,128)(2,1)S(1)} %get-tuple-element.21, bf16[2048,1,3,768]{3,0,2,1:T(8,128)(2,1)} %all-gather.2.cloned.1.call-done), kind=kOutput, calls=%fused_computation.24 | convolution fusion | flops 302186496 | bytes 3686400 | tf_op jit(solution)/shard_map/sjcf,djf->sjcd/dot_general | solution.py:46
  179.1 3.7 %all-to-all-done.3 = bf16[4,1,24,2048]{3,2,1,0:T(8,128)(2,1)S(1)} async-done(((bf16[4,1,24,2048]{3,2,1,0:T(8,128)(2,1)}), bf16[4,1,24,2048]{3,2,1,0:T(8,128)(2,1)S(1)}, u32[]{:S(2)}, u32[]{:S(2)}) %all-to-all-start.3) | async-done | bytes 393248 | tf_op jit(solution)/shard_map/all_to_all | solution.py:64
  182.8 3.5 %all-to-all-start.1 = ((bf16[4,1,24,2048]{3,2,1,0:T(8,128)(2,1)}), bf16[4,1,24,2048]{3,2,1,0:T(8,128)(2,1)S(1)}, u32[]{:S(2)}, u32[]{:S(2)}) async-start(bf16[4,1,24,2048]{3,2,1,0:T(8,128)(2,1)} %fusion.13), calls=%async_computation.1 | async-start | bytes 786432 | tf_op jit(solution)/shard_map/all_to_all | solution.py:63
  186.3 1.8 bitcast_convert_fusion.3
  188.1 5.6 %all-to-all-done.1 = bf16[4,1,24,2048]{3,2,1,0:T(8,128)(2,1)S(1)} async-done(((bf16[4,1,24,2048]{3,2,1,0:T(8,128)(2,1)}), bf16[4,1,24,2048]{3,2,1,0:T(8,128)(2,1)S(1)}, u32[]{:S(2)}, u32[]{:S(2)}) %all-to-all-start.1) | async-done | bytes 393248 | tf_op jit(solution)/shard_map/all_to_all | solution.py:63
  193.6 0.6 fusion.35
  194.3 0.6 fusion.36
  194.9 0.6 fusion.37
  195.5 2.4 add_convert_fusion
  197.9 128.0 %reduce-scatter.2.cloned.1.call-done = bf16[256,1,3,768]{0,3,2,1:T(8,128)(2,1)} async-done(((bf16[2048,1,3,768]{0,3,2,1:T(8,128)(2,1)}), bf16[256,1,3,768]{0,3,2,1:T(8,128)(2,1)}) %reduce-scatter.2.cloned.1.call-update) | async-done | bytes 1179664 | tf_op jit(solution)/shard_map/reduce_scatter | solution.py:70
  325.9 6.3 %copy.28 = f32[256,1,3,768]{3,1,2,0:T(1,128)} copy(bf16[256,1,3,768]{0,3,2,1:T(8,128)(2,1)} %reduce-scatter.2.cloned.1.call-done) | data formatting | bytes 3538944
  (21 shorter events, 0.8 us)
Async XLA Ops:
  7.2 5.0 %copy-start = (bf16[384,2048]{1,0:T(8,128)(2,1)S(1)}, bf16[384,2048]{1,0:T(8,128)(2,1)}, u32[]{:S(2)}) copy-start(bf16[384,2048]{1,0:T(8,128)(2,1)} %param.8) | copy-start | bytes 4718596
  7.2 10.4 %copy-start.1 = (bf16[384,2048]{1,0:T(8,128)(2,1)S(1)}, bf16[384,2048]{1,0:T(8,128)(2,1)}, u32[]{:S(2)}) copy-start(bf16[384,2048]{1,0:T(8,128)(2,1)} %param.5) | copy-start | bytes 4718596
  7.2 143.0 %all-gather.2.cloned.1.call-start = ((), (), s32[]{:S(2)}) async-start(), calls=%async_computation.5 | async-start | bytes 10616832 | tf_op jit(solution)/shard_map/all_gather | solution.py:36
  12.0 1.3 copy-start.2
  13.3 11.6 %all-to-all-start.2 = ((bf16[4,1,24,2048]{3,2,1,0:T(8,128)(2,1)}), bf16[4,1,24,2048]{3,2,1,0:T(8,128)(2,1)S(1)}, u32[]{:S(2)}, u32[]{:S(2)}) async-start(bf16[4,1,24,2048]{3,2,1,0:T(8,128)(2,1)} %fusion.16), calls=%async_computation.2 | async-start | bytes 786432 | tf_op jit(solution)/shard_map/all_to_all | solution.py:34
  25.0 127.7 %all-to-all-start = ((bf16[4,1,24,2048]{3,2,1,0:T(8,128)(2,1)}), bf16[4,1,24,2048]{3,2,1,0:T(8,128)(2,1)S(1)}, u32[]{:S(2)}, u32[]{:S(2)}) async-start(bf16[4,1,24,2048]{3,2,1,0:T(8,128)(2,1)} %fusion.14), calls=%async_computation | async-start | bytes 786432 | tf_op jit(solution)/shard_map/all_to_all | solution.py:33
  28.5 297.5 %reduce-scatter.2.cloned.1.call-start = ((), (), s32[]{:S(2)}) async-start(), calls=%async_computation.6 | async-start | bytes 10616832 | tf_op jit(solution)/shard_map/reduce_scatter | solution.py:70
  171.8 14.5 %copy-start.3 = (f32[384,4]{0,1:T(4,128)S(1)}, f32[384,4]{0,1:T(4,128)}, u32[]{:S(2)}) copy-start(f32[384,4]{0,1:T(4,128)} %copy-done.2) | copy-start | bytes 18436
  171.8 11.0 %all-to-all-start.3 = ((bf16[4,1,24,2048]{3,2,1,0:T(8,128)(2,1)}), bf16[4,1,24,2048]{3,2,1,0:T(8,128)(2,1)S(1)}, u32[]{:S(2)}, u32[]{:S(2)}) async-start(bf16[4,1,24,2048]{3,2,1,0:T(8,128)(2,1)} %fusion.15), calls=%async_computation.3 | async-start | bytes 786432 | tf_op jit(solution)/shard_map/all_to_all | solution.py:64
  182.8 10.8 %all-to-all-start.1 = ((bf16[4,1,24,2048]{3,2,1,0:T(8,128)(2,1)}), bf16[4,1,24,2048]{3,2,1,0:T(8,128)(2,1)S(1)}, u32[]{:S(2)}, u32[]{:S(2)}) async-start(bf16[4,1,24,2048]{3,2,1,0:T(8,128)(2,1)} %fusion.13), calls=%async_computation.1 | async-start | bytes 786432 | tf_op jit(solution)/shard_map/all_to_all | solution.py:63
Sparse Core Ops, SparseCore 0:
  10.2 139.9 all-gather.1
  165.2 160.6 reduce-scatter.1
where the time goes:
time: 340 us; the launch traced here: 339 us
  waiting for transfers between devices  266 us (78%)
  matrix products  29.5 us (9%)
  starting transfers between devices  14.8 us (4%)
  between operations  14.2 us (4%)
  other arithmetic  8.13 us (2%)
  local copies, waits for them, and re-layouts  6.59 us (2%)
    reduce_scatter x1, waiting for transfers between devices, body(): lax.psum_scatter(full_terms.astype(jnp.bfloat16), 'ctx', scatter_dimensio...  128 us
    all_gather x1, waiting for transfers between devices, body(): gathered = lax.all_gather(expert_weights, 'ctx', axis=0, tiled=True)  122 us
  transfers between devices with their start and end apart: 6, of which 5 were waited for; matrix products, arithmetic and copies ran while one was open for 8% of the time, Pallas kernels for 0%

commit v1 on v0

v1 whole, which is shorter than its diff:
```python
import jax
import jax.numpy as jnp
from jax import lax
from jax.sharding import PartitionSpec as P

CAP = 24
F32 = jnp.float32
BF16 = jnp.bfloat16


def dot_nn(a, b):
    return lax.dot_general(a, b, (((1,), (0,)), ((), ())), preferred_element_type=F32)


def dot_nt(a, b):
    return lax.dot_general(a, b, (((1,), (1,)), ((), ())), preferred_element_type=F32)


def dot_tn(a, b):
    return lax.dot_general(a, b, (((0,), (0,)), ((), ())), preferred_element_type=F32)


def body(tokens, expert_ids, gate_codes, out_grad, expert_weights):
    n_ep = lax.axis_size("ep")
    n_ctx = lax.axis_size("ctx")
    n_hi = n_ctx // 2
    n_tok, width = tokens.shape
    d_own, _, _, ff = expert_weights.shape
    rows = n_ep * CAP
    odd = lax.axis_index("ctx") % 2 == 1
    pair = [(c, c ^ 1) for c in range(n_ctx)]
    lines = [[2 * h + low for h in range(n_hi)] for low in range(2)]

    def swap(x):
        return lax.ppermute(x, "ctx", pair)

    def over_line(x):
        return lax.all_to_all(
            x, "ctx", split_axis=0, concat_axis=0, axis_index_groups=lines, tiled=True
        )

    def over_ep(x):
        return lax.all_to_all(x, "ep", split_axis=0, concat_axis=0, tiled=True)

    own = [expert_weights[:, 0, k, :] for k in range(3)]
    peer = [None] * 3
    for k in (2, 0, 1):
        peer[k] = swap(own[k])

    gates = gate_codes.astype(F32) / 65536.0
    wave_range = jnp.arange(n_ep, dtype=jnp.int32)
    chosen = expert_ids[:, :, None] == wave_range[None, None, :]
    member = jnp.any(chosen, axis=1)
    route_weight = jnp.sum(jnp.where(chosen, gates[:, :, None], 0.0), axis=1)
    position = jnp.cumsum(member.astype(jnp.int32), axis=0) - 1
    placed = member[:, :, None] & (
        position[:, :, None] == jnp.arange(CAP, dtype=jnp.int32)[None, None, :]
    )
    onehot = placed.astype(BF16).reshape(n_tok, rows)
    slot_weight = jnp.sum(jnp.where(placed, route_weight[:, :, None], 0.0), axis=0)

    def arrange(x):
        x = x.reshape(rows, n_hi, 2, d_own)
        x = jnp.where(odd, x[:, :, ::-1, :], x)
        return x.reshape(rows, n_hi, 2 * d_own)

    def dispatch(x):
        x = over_ep(arrange(x))
        x = over_line(jnp.transpose(x, (1, 0, 2)))
        return x.reshape(n_hi * rows, 2 * d_own)

    slot_grad = (slot_weight.reshape(rows, 1) * dot_tn(onehot, out_grad)).astype(BF16)
    slot_rows = dot_tn(onehot, tokens).astype(BF16)
    g_all = dispatch(slot_grad)
    x_all = dispatch(slot_rows)

    def partial_sum(a, k):
        part = dot_nn(a[:, :d_own], own[k]) + dot_nn(a[:, d_own:], peer[k])
        part = over_line(part.astype(BF16).reshape(n_hi, rows, ff))
        return jnp.sum(part.astype(F32), axis=0)

    hidden_grad = partial_sum(g_all, 2)
    pre_gate = partial_sum(x_all, 0)
    pre_up = partial_sum(x_all, 1)
    soft = jax.nn.sigmoid(pre_gate)
    active = pre_gate * soft
    hidden = (active * pre_up).astype(BF16)
    gate_grad = (hidden_grad * pre_up * soft * (1.0 + pre_gate * (1.0 - soft))).astype(BF16)
    up_grad = (hidden_grad * active).astype(BF16)

    def gather(x):
        x = jnp.broadcast_to(x[None], (n_hi, rows, ff))
        return over_line(x).reshape(n_hi * rows, ff)

    hidden_all = gather(hidden)
    gate_all = gather(gate_grad)
    up_all = gather(up_grad)

    x_own, x_peer = x_all[:, :d_own], x_all[:, d_own:]
    g_own, g_peer = g_all[:, :d_own], g_all[:, d_own:]

    def give_back(first, second):
        x = jnp.concatenate([first, second], axis=1).astype(BF16)
        x = over_line(x.reshape(n_hi, rows, 2 * d_own))
        x = over_ep(jnp.transpose(x, (1, 0, 2)))
        x = x.reshape(rows, n_hi, 2, d_own)
        x = jnp.where(odd, x[:, :, ::-1, :], x)
        return x.reshape(rows, width)

    out_back = give_back(dot_nt(hidden_all, own[2]), dot_nt(hidden_all, peer[2]))
    down_peer = swap(dot_tn(g_peer, hidden_all).astype(BF16))
    input_back = give_back(
        dot_nt(gate_all, own[0]) + dot_nt(up_all, own[1]),
        dot_nt(gate_all, peer[0]) + dot_nt(up_all, peer[1]),
    )
    gate_peer = swap(dot_tn(x_peer, gate_all).astype(BF16))
    up_peer = swap(dot_tn(x_peer, up_all).astype(BF16))
    weight_grads = jnp.stack(
        [
            dot_tn(x_own, gate_all) + gate_peer.astype(F32),
            dot_tn(x_own, up_all) + up_peer.astype(F32),
            dot_tn(g_own, hidden_all) + down_peer.astype(F32),
        ],
        axis=1,
    )[:, None]

    combined = jnp.zeros((n_tok, width), F32)
    for expert in range(n_ep):
        part = slice(expert * CAP, (expert + 1) * CAP)
        picked = dot_nn(onehot[:, part], out_back[part])
        combined = combined + route_weight[:, expert : expert + 1] * picked
    input_grad = dot_nn(onehot, input_back)
    return combined.astype(BF16), input_grad.astype(BF16), weight_grads


def solution(mesh):
    by_token = P(("ctx", "ep"), None)
    by_weight = P("ctx", "ep", None, None)
    return jax.shard_map(
        body,
        mesh=mesh,
        in_specs=(by_token, by_token, by_token, by_token, by_weight),
        out_specs=(by_token, by_token, by_weight),
        check_vma=False,
    )
```

time: 340 us -> 257 us (0.76)
  waiting for transfers between devices: 266 us -> 94 us
  starting transfers between devices: 14.8 us -> 60.3 us
  local copies, waits for them, and re-layouts: 6.59 us -> 30.9 us
  blocking collectives: 0 us -> 17.8 us
  between operations: 14.2 us -> 1.13 us
  matrix products: 29.5 us -> 39.9 us
    reduce_scatter x1 -> x0, waiting for transfers between devices: 128 us -> none  [body(): lax.psum_scatter(full_terms.astype(jnp.bfloat16), 'ctx', scatter_dimensio...]
    all_gather x1 -> x0, waiting for transfers between devices: 122 us -> none  [body(): gathered = lax.all_gather(expert_weights, 'ctx', axis=0, tiled=True)]
    all_to_all x4 -> x13, waiting for transfers between devices: 15.5 us -> 77 us  [the longest x9 69.4 us: over_line(): lax.all_to_all(x, 'ctx', split_axis=0, concat_axis=0, axis_index_groups=l...]
    all_to_all x4 -> x13, starting transfers between devices: 14.7 us -> 52.1 us  [the longest x9 36 us: over_line(): lax.all_to_all(x, 'ctx', split_axis=0, concat_axis=0, axis_index_groups=l...]
    all_to_all x0 -> x1, blocking collectives: none -> 17.8 us  [over_line(): lax.all_to_all(x, 'ctx', split_axis=0, concat_axis=0, axis_index_groups=l...]
    ppermute x0 -> x6, waiting for transfers between devices: none -> 17 us  [swap(): return lax.ppermute(x, 'ctx', pair)]
    dot_general x16 -> x25, matrix products: 29.5 us -> 39.9 us  [the longest x11 20.7 us: dot_nn(): lax.dot_general(a, b, (((1,), (0,)), ((), ())), preferred_element_type=F32)]
    rev x0 -> x4, local copies, waits for them, and re-layouts: none -> 8.33 us  [the longest x2 4.17 us: arrange(): x = jnp.where(odd, x[:, :, ::-1, :], x)]
  transfers between devices with their start and end apart: 6 -> 19, of which waited for: 5 -> 14; matrix products, arithmetic and copies ran while one was open for 8% -> 20% of each run, Pallas kernels for 0% -> 0%
where the time goes in v1:
time: 257 us; the launch traced here: 255 us
  waiting for transfers between devices  94 us (37%)
  starting transfers between devices  60.3 us (23%)
  matrix products  39.9 us (16%)
  local copies, waits for them, and re-layouts  30.9 us (12%)
  blocking collectives  17.8 us (7%)
  other arithmetic  11.2 us (4%)
    all_to_all x9, waiting for transfers between devices, over_line(): lax.all_to_all(x, 'ctx', split_axis=0, concat_axis=0, axis_index_groups=l...  69.4 us
    all_to_all x9, starting transfers between devices, over_line(): lax.all_to_all(x, 'ctx', split_axis=0, concat_axis=0, axis_index_groups=l...  36 us
    dot_general x11, matrix products, dot_nn(): lax.dot_general(a, b, (((1,), (0,)), ((), ())), preferred_element_type=F32)  20.7 us
    all_to_all x1, blocking collectives, over_line(): lax.all_to_all(x, 'ctx', split_axis=0, concat_axis=0, axis_index_groups=l...  17.8 us
    ppermute x6, waiting for transfers between devices, swap(): return lax.ppermute(x, 'ctx', pair)  17 us
    all_to_all x4, starting transfers between devices, over_ep(): return lax.all_to_all(x, 'ep', split_axis=0, concat_axis=0, tiled=True)  16.1 us
    dot_general x8, matrix products, dot_tn(): lax.dot_general(a, b, (((0,), (0,)), ((), ())), preferred_element_type=F32)  11.9 us
    ppermute x6, starting transfers between devices, swap(): return lax.ppermute(x, 'ctx', pair)  8.25 us
  transfers between devices with their start and end apart: 19, of which 14 were waited for; matrix products, arithmetic and copies ran while one was open for 20% of the time, Pallas kernels for 0%

profile of v1, /device:TPU:0, one launch (start us, length us, event | category | flops | bytes accessed | tf_op | source)
XLA Modules:
  0.0 255.3 jit_solution(4666362793405870187)
XLA Ops:
  9.0 4.2 %all-to-all-start.7 = ((bf16[96,4,512]{2,1,0:T(4,128)(2,1)}), bf16[96,4,512]{2,1,0:T(4,128)(2,1)S(1)}, u32[]{:S(2)}, u32[]{:S(2)}) async-start(bf16[96,4,512]{2,1,0:T(4,128)(2,1)} %reshape.164), calls=%async_computation.7 | async-start | bytes 786432 | tf_op jit(solution)/shard_map/all_to_all | solution.py:43
  20.6 3.5 %all-to-all-start = ((bf16[96,4,512]{2,1,0:T(4,128)(2,1)}), bf16[96,4,512]{2,1,0:T(4,128)(2,1)S(1)}, u32[]{:S(2)}, u32[]{:S(2)}) async-start(bf16[96,4,512]{2,1,0:T(4,128)(2,1)} %reshape.158), calls=%async_computation | async-start | bytes 786432 | tf_op jit(solution)/shard_map/all_to_all | solution.py:43
  24.9 6.6 %all-to-all-done = bf16[96,4,512]{2,1,0:T(4,128)(2,1)S(1)} async-done(((bf16[96,4,512]{2,1,0:T(4,128)(2,1)}), bf16[96,4,512]{2,1,0:T(4,128)(2,1)S(1)}, u32[]{:S(2)}, u32[]{:S(2)}) %all-to-all-start) | async-done | bytes 393248 | tf_op jit(solution)/shard_map/all_to_all | solution.py:43
  31.5 5.5 %all-to-all-start.8 = ((bf16[4,96,512]{2,1,0:T(8,128)(2,1)}), bf16[4,96,512]{2,1,0:T(8,128)(2,1)S(1)}, u32[]{:S(2)}, u32[]{:S(2)}) async-start(bf16[4,96,512]{2,1,0:T(8,128)(2,1)} %bitcast.132), calls=%async_computation.8 | async-start | bytes 786432 | tf_op jit(solution)/shard_map/all_to_all | solution.py:38
  40.4 8.0 %all-to-all-done.8 = bf16[4,96,512]{2,1,0:T(8,128)(2,1)S(1)} async-done(((bf16[4,96,512]{2,1,0:T(8,128)(2,1)}), bf16[4,96,512]{2,1,0:T(8,128)(2,1)S(1)}, u32[]{:S(2)}, u32[]{:S(2)}) %all-to-all-start.8) | async-done | bytes 393248 | tf_op jit(solution)/shard_map/all_to_all | solution.py:38
  48.4 3.5 %all-to-all-start.1 = ((bf16[4,96,512]{2,1,0:T(8,128)(2,1)}), bf16[4,96,512]{2,1,0:T(8,128)(2,1)S(1)}, u32[]{:S(2)}, u32[]{:S(2)}) async-start(bf16[4,96,512]{2,1,0:T(8,128)(2,1)} %bitcast.133), calls=%async_computation.1 | async-start | bytes 786432 | tf_op jit(solution)/shard_map/all_to_all | solution.py:38
  54.3 8.7 %all-to-all-done.1 = bf16[4,96,512]{2,1,0:T(8,128)(2,1)S(1)} async-done(((bf16[4,96,512]{2,1,0:T(8,128)(2,1)}), bf16[4,96,512]{2,1,0:T(8,128)(2,1)S(1)}, u32[]{:S(2)}, u32[]{:S(2)}) %all-to-all-start.1) | async-done | bytes 393248 | tf_op jit(solution)/shard_map/all_to_all | solution.py:38
  63.1 4.2 %all-to-all-start.9 = ((bf16[4,96,768]{2,1,0:T(8,128)(2,1)}), bf16[4,96,768]{2,1,0:T(8,128)(2,1)}, u32[]{:S(2)}, u32[]{:S(2)}) async-start(bf16[4,96,768]{2,1,0:T(8,128)(2,1)} %bitcast.130), calls=%async_computation.9 | async-start | bytes 1179648 | tf_op jit(solution)/shard_map/all_to_all | solution.py:38
  69.1 8.5 %collective-permute-done.1 = bf16[256,768]{1,0:T(8,128)(2,1)S(1)} collective-permute-done((bf16[256,768]{1,0:T(8,128)(2,1)}, bf16[256,768]{1,0:T(8,128)(2,1)S(1)}, u32[]{:S(2)}, u32[]{:S(2)}) %collective-permute-start.1) | collective-permute-done | bytes 393248 | tf_op jit(solution)/shard_map/ppermute | solution.py:35
  79.5 3.2 %all-to-all-done.9 = bf16[4,96,768]{2,1,0:T(8,128)(2,1)} async-done(((bf16[4,96,768]{2,1,0:T(8,128)(2,1)}), bf16[4,96,768]{2,1,0:T(8,128)(2,1)}, u32[]{:S(2)}, u32[]{:S(2)}) %all-to-all-start.9) | async-done | bytes 589856 | tf_op jit(solution)/shard_map/all_to_all | solution.py:38
  82.7 4.1 %all-to-all-start.3 = ((bf16[4,96,768]{2,1,0:T(8,128)(2,1)}), bf16[4,96,768]{2,1,0:T(8,128)(2,1)}, u32[]{:S(2)}, u32[]{:S(2)}) async-start(bf16[4,96,768]{2,1,0:T(8,128)(2,1)} %bitcast.129), calls=%async_computation.3 | async-start | bytes 1179648 | tf_op jit(solution)/shard_map/all_to_all | solution.py:38
  88.8 8.5 %collective-permute-done = bf16[256,768]{1,0:T(8,128)(2,1)S(1)} collective-permute-done((bf16[256,768]{1,0:T(8,128)(2,1)}, bf16[256,768]{1,0:T(8,128)(2,1)S(1)}, u32[]{:S(2)}, u32[]{:S(2)}) %collective-permute-start) | collective-permute-done | bytes 393248 | tf_op jit(solution)/shard_map/ppermute | solution.py:35
  99.2 3.2 %all-to-all-done.3 = bf16[4,96,768]{2,1,0:T(8,128)(2,1)} async-done(((bf16[4,96,768]{2,1,0:T(8,128)(2,1)}), bf16[4,96,768]{2,1,0:T(8,128)(2,1)}, u32[]{:S(2)}, u32[]{:S(2)}) %all-to-all-start.3) | async-done | bytes 589856 | tf_op jit(solution)/shard_map/all_to_all | solution.py:38
  102.4 3.5 %all-to-all-start.2 = ((bf16[4,96,768]{2,1,0:T(8,128)(2,1)}), bf16[4,96,768]{2,1,0:T(8,128)(2,1)S(1)}, u32[]{:S(2)}, u32[]{:S(2)}) async-start(bf16[4,96,768]{2,1,0:T(8,128)(2,1)} %bitcast.8), calls=%async_computation.2 | async-start | bytes 1179648 | tf_op jit(solution)/shard_map/all_to_all | solution.py:38
  108.2 13.1 %all-to-all-done.2 = bf16[4,96,768]{2,1,0:T(8,128)(2,1)S(1)} async-done(((bf16[4,96,768]{2,1,0:T(8,128)(2,1)}), bf16[4,96,768]{2,1,0:T(8,128)(2,1)S(1)}, u32[]{:S(2)}, u32[]{:S(2)}) %all-to-all-start.2) | async-done | bytes 589856 | tf_op jit(solution)/shard_map/all_to_all | solution.py:38
  122.2 17.8 %all_to_all.70 = bf16[4,96,768]{2,1,0:T(8,128)(2,1)S(1)} all-to-all(bf16[4,96,768]{2,1,0:T(8,128)(2,1)S(1)} %broadcast_in_dim.34), channel_id=1, replica_groups={{0,8,16,24},{4,12,20,28},{1,9,17,25},{5,13,21,29},{2,10,18,26},{6,14,22..., dimensions={0} | all-to-all | bytes 1179648 | tf_op jit(solution)/shard_map/all_to_all | solution.py:38
  141.0 3.5 %all-to-all-start.10 = ((bf16[4,96,768]{2,1,0:T(8,128)(2,1)}), bf16[4,96,768]{2,1,0:T(8,128)(2,1)S(1)}, u32[]{:S(2)}, u32[]{:S(2)}) async-start(bf16[4,96,768]{2,1,0:T(8,128)(2,1)} %broadcast_in_dim.57), calls=%async_computation.10 | async-start | bytes 1179648 | tf_op jit(solution)/shard_map/all_to_all | solution.py:38
  148.5 11.2 %all-to-all-done.10 = bf16[4,96,768]{2,1,0:T(8,128)(2,1)S(1)} async-done(((bf16[4,96,768]{2,1,0:T(8,128)(2,1)}), bf16[4,96,768]{2,1,0:T(8,128)(2,1)S(1)}, u32[]{:S(2)}, u32[]{:S(2)}) %all-to-all-start.10) | async-done | bytes 589856 | tf_op jit(solution)/shard_map/all_to_all | solution.py:38
  161.4 3.5 %all-to-all-start.11 = ((bf16[4,96,768]{2,1,0:T(8,128)(2,1)}), bf16[4,96,768]{2,1,0:T(8,128)(2,1)S(1)}, u32[]{:S(2)}, u32[]{:S(2)}) async-start(bf16[4,96,768]{2,1,0:T(8,128)(2,1)} %broadcast_in_dim.58), calls=%async_computation.11 | async-start | bytes 1179648 | tf_op jit(solution)/shard_map/all_to_all | solution.py:38
  170.8 9.5 %all-to-all-done.11 = bf16[4,96,768]{2,1,0:T(8,128)(2,1)S(1)} async-done(((bf16[4,96,768]{2,1,0:T(8,128)(2,1)}), bf16[4,96,768]{2,1,0:T(8,128)(2,1)S(1)}, u32[]{:S(2)}, u32[]{:S(2)}) %all-to-all-start.11) | async-done | bytes 589856 | tf_op jit(solution)/shard_map/all_to_all | solution.py:38
  180.3 4.1 %all-to-all-start.5 = ((bf16[4,96,512]{2,1,0:T(8,128)(2,1)}), bf16[4,96,512]{2,1,0:T(8,128)(2,1)}, u32[]{:S(2)}, u32[]{:S(2)}) async-start(bf16[4,96,512]{2,1,0:T(8,128)(2,1)} %pad_maximum_fusion), calls=%async_computation.5 | async-start | bytes 786432 | tf_op jit(solution)/shard_map/all_to_all | solution.py:38
  187.5 8.2 %all-to-all-done.5 = bf16[4,96,512]{2,1,0:T(8,128)(2,1)} async-done(((bf16[4,96,512]{2,1,0:T(8,128)(2,1)}), bf16[4,96,512]{2,1,0:T(8,128)(2,1)}, u32[]{:S(2)}, u32[]{:S(2)}) %all-to-all-start.5) | async-done | bytes 393248 | tf_op jit(solution)/shard_map/all_to_all | solution.py:38
  195.7 4.1 %all-to-all-start.12 = ((bf16[4,96,512]{2,1,0:T(8,128)(2,1)}), bf16[4,96,512]{2,1,0:T(8,128)(2,1)}, u32[]{:S(2)}, u32[]{:S(2)}) async-start(bf16[4,96,512]{2,1,0:T(8,128)(2,1)} %pad_maximum_fusion.1), calls=%async_computation.12 | async-start | bytes 786432 | tf_op jit(solution)/shard_map/all_to_all | solution.py:38
  206.9 4.3 %all-to-all-done.12 = bf16[4,96,512]{2,1,0:T(8,128)(2,1)} async-done(((bf16[4,96,512]{2,1,0:T(8,128)(2,1)}), bf16[4,96,512]{2,1,0:T(8,128)(2,1)}, u32[]{:S(2)}, u32[]{:S(2)}) %all-to-all-start.12) | async-done | bytes 393248 | tf_op jit(solution)/shard_map/all_to_all | solution.py:38
  211.1 4.1 %all-to-all-start.6 = ((bf16[96,4,512]{2,1,0:T(4,128)(2,1)}), bf16[96,4,512]{2,1,0:T(4,128)(2,1)}, u32[]{:S(2)}, u32[]{:S(2)}) async-start(bf16[96,4,512]{2,1,0:T(4,128)(2,1)} %copy.44), calls=%async_computation.6 | async-start | bytes 786432 | tf_op jit(solution)/shard_map/all_to_all | solution.py:43
  215.3 2.4 add_bitcast_fusion
  222.7 4.3 %all-to-all-start.13 = ((bf16[96,4,512]{2,1,0:T(4,128)(2,1)}), bf16[96,4,512]{2,1,0:T(4,128)(2,1)}, u32[]{:S(2)}, u32[]{:S(2)}) async-start(bf16[96,4,512]{2,1,0:T(4,128)(2,1)} %copy.46), calls=%async_computation.13 | async-start | bytes 786432 | tf_op jit(solution)/shard_map/all_to_all | solution.py:43
  228.7 3.8 %copy.47 = f32[256,1,3,768]{3,1,2,0:T(1,128)} copy(f32[256,1,3,768]{3,0,2,1:T(8,128)S(1)} %maximum_bitcast_fusion) | data formatting | bytes 4718592
  239.5 3.0 %fusion.40 = f32[384,2048]{1,0:T(8,128)} fusion(bf16[24,2048]{1,0:T(8,128)(2,1)S(1)} %slice.95, pred[384,96]{0,1:T(8,128)(4,1)} %copy-done.9), kind=kOutput, calls=%fused_computation.75 | convolution fusion | flops 37748736 | bytes 3253248 | tf_op jit(solution)/shard_map/dot_general | solution.py:12
  242.5 2.3 fusion.42
  244.9 2.3 fusion.38
  249.4 5.9 %add_convert_fusion = bf16[384,2048]{1,0:T(8,128)(2,1)} fusion(f32[384,2048]{1,0:T(8,128)} %fusion.38, f32[384,2048]{1,0:T(8,128)} %fusion.40, f32[384,2048]{1,0:T(8,128)} %fusion.42, bf16[24,2048]{1,0:T(8,128)(2,1)S(1)} %slice.103, f32[384]{0:T(512)S(1)} %get-tuple-element.19, f32[384]{0:T(512)S(1)} %copy-done.13, f32[384]{0:T(512)S(1)} %copy-done.14, ...), kind=kOutput, calls=%fused_computation | convolution fusion | flops 44040192 | bytes 11125760 | tf_op jit(solution)/shard_map/dot_general | solution.py:12
  (114 shorter events, 71.4 us)
Async XLA Ops:
  0.6 4.5 %copy-start = (bf16[384,2048]{1,0:T(8,128)(2,1)S(1)}, bf16[384,2048]{1,0:T(8,128)(2,1)}, u32[]{:S(2)}) copy-start(bf16[384,2048]{1,0:T(8,128)(2,1)} %param.8) | copy-start | bytes 4718596
  1.5 6.4 %copy-start.12 = (pred[384,4]{0,1:T(4,128)(4,1)}, pred[384,4]{0,1:T(4,128)(4,1)S(1)}, u32[]{:S(2)}) copy-start(pred[384,4]{0,1:T(4,128)(4,1)S(1)} %fusion.36) | copy-start | bytes 4612
  4.9 8.3 %copy-start.9 = (pred[384,96]{0,1:T(8,128)(4,1)}, pred[384,96]{0,1:T(8,128)(4,1)S(1)}, u32[]{:S(2)}) copy-start(pred[384,96]{0,1:T(8,128)(4,1)S(1)} %fusion.19) | copy-start | bytes 110596
  9.0 11.6 %all-to-all-start.7 = ((bf16[96,4,512]{2,1,0:T(4,128)(2,1)}), bf16[96,4,512]{2,1,0:T(4,128)(2,1)S(1)}, u32[]{:S(2)}, u32[]{:S(2)}) async-start(bf16[96,4,512]{2,1,0:T(4,128)(2,1)} %reshape.164), calls=%async_computation.7 | async-start | bytes 786432 | tf_op jit(solution)/shard_map/all_to_all | solution.py:43
  18.2 18.8 %copy-start.2 = (bf16[256,1,3,768]{3,0,2,1:T(8,128)(2,1)S(1)}, bf16[256,1,3,768]{3,0,2,1:T(8,128)(2,1)}, u32[]{:S(2)}) copy-start(bf16[256,1,3,768]{3,0,2,1:T(8,128)(2,1)} %param.9) | copy-start | bytes 3538948
  20.6 10.8 %all-to-all-start = ((bf16[96,4,512]{2,1,0:T(4,128)(2,1)}), bf16[96,4,512]{2,1,0:T(4,128)(2,1)S(1)}, u32[]{:S(2)}, u32[]{:S(2)}) async-start(bf16[96,4,512]{2,1,0:T(4,128)(2,1)} %reshape.158), calls=%async_computation | async-start | bytes 786432 | tf_op jit(solution)/shard_map/all_to_all | solution.py:43
  31.5 16.9 %all-to-all-start.8 = ((bf16[4,96,512]{2,1,0:T(8,128)(2,1)}), bf16[4,96,512]{2,1,0:T(8,128)(2,1)S(1)}, u32[]{:S(2)}, u32[]{:S(2)}) async-start(bf16[4,96,512]{2,1,0:T(8,128)(2,1)} %bitcast.132), calls=%async_computation.8 | async-start | bytes 786432 | tf_op jit(solution)/shard_map/all_to_all | solution.py:38
  38.0 14.2 %collective-permute-start.2 = (bf16[256,768]{1,0:T(8,128)(2,1)}, bf16[256,768]{1,0:T(8,128)(2,1)}, u32[]{:S(2)}, u32[]{:S(2)}) collective-permute-start(bf16[256,768]{1,0:T(8,128)(2,1)} %get-tuple-element.22), channel_id=1, source_target_pairs={{0,4},{4,0},{8,12},{12,8},{16,20},{20,16},{24,28},{28,24},{1,5},{5... | collective-permute-start | bytes 1179656 | tf_op jit(solution)/shard_map/ppermute | solution.py:35
  48.4 14.7 %all-to-all-start.1 = ((bf16[4,96,512]{2,1,0:T(8,128)(2,1)}), bf16[4,96,512]{2,1,0:T(8,128)(2,1)S(1)}, u32[]{:S(2)}, u32[]{:S(2)}) async-start(bf16[4,96,512]{2,1,0:T(8,128)(2,1)} %bitcast.133), calls=%async_computation.1 | async-start | bytes 786432 | tf_op jit(solution)/shard_map/all_to_all | solution.py:38
  63.1 19.7 %all-to-all-start.9 = ((bf16[4,96,768]{2,1,0:T(8,128)(2,1)}), bf16[4,96,768]{2,1,0:T(8,128)(2,1)}, u32[]{:S(2)}, u32[]{:S(2)}) async-start(bf16[4,96,768]{2,1,0:T(8,128)(2,1)} %bitcast.130), calls=%async_computation.9 | async-start | bytes 1179648 | tf_op jit(solution)/shard_map/all_to_all | solution.py:38
  67.2 10.4 %collective-permute-start.1 = (bf16[256,768]{1,0:T(8,128)(2,1)}, bf16[256,768]{1,0:T(8,128)(2,1)S(1)}, u32[]{:S(2)}, u32[]{:S(2)}) collective-permute-start(bf16[256,768]{1,0:T(8,128)(2,1)} %get-tuple-element.24), channel_id=1, source_target_pairs={{0,4},{4,0},{8,12},{12,8},{16,20},{20,16},{24,28},{28,24},{1,5},{5... | collective-permute-start | bytes 1179656 | tf_op jit(solution)/shard_map/ppermute | solution.py:35
  82.7 19.7 %all-to-all-start.3 = ((bf16[4,96,768]{2,1,0:T(8,128)(2,1)}), bf16[4,96,768]{2,1,0:T(8,128)(2,1)}, u32[]{:S(2)}, u32[]{:S(2)}) async-start(bf16[4,96,768]{2,1,0:T(8,128)(2,1)} %bitcast.129), calls=%async_computation.3 | async-start | bytes 1179648 | tf_op jit(solution)/shard_map/all_to_all | solution.py:38
  86.9 10.4 %collective-permute-start = (bf16[256,768]{1,0:T(8,128)(2,1)}, bf16[256,768]{1,0:T(8,128)(2,1)S(1)}, u32[]{:S(2)}, u32[]{:S(2)}) collective-permute-start(bf16[256,768]{1,0:T(8,128)(2,1)} %get-tuple-element.23), channel_id=1, source_target_pairs={{0,4},{4,0},{8,12},{12,8},{16,20},{20,16},{24,28},{28,24},{1,5},{5... | collective-permute-start | bytes 1179656 | tf_op jit(solution)/shard_map/ppermute | solution.py:35
  102.4 18.9 %all-to-all-start.2 = ((bf16[4,96,768]{2,1,0:T(8,128)(2,1)}), bf16[4,96,768]{2,1,0:T(8,128)(2,1)S(1)}, u32[]{:S(2)}, u32[]{:S(2)}) async-start(bf16[4,96,768]{2,1,0:T(8,128)(2,1)} %bitcast.8), calls=%async_computation.2 | async-start | bytes 1179648 | tf_op jit(solution)/shard_map/all_to_all | solution.py:38
  140.1 19.6 %copy-start.1 = (bf16[4,96,768]{2,1,0:T(8,128)(2,1)}, bf16[4,96,768]{2,1,0:T(8,128)(2,1)S(1)}, u32[]{:S(2)}) copy-start(bf16[4,96,768]{2,1,0:T(8,128)(2,1)S(1)} %all_to_all.70) | copy-start | bytes 1769476
  141.0 18.6 %all-to-all-start.10 = ((bf16[4,96,768]{2,1,0:T(8,128)(2,1)}), bf16[4,96,768]{2,1,0:T(8,128)(2,1)S(1)}, u32[]{:S(2)}, u32[]{:S(2)}) async-start(bf16[4,96,768]{2,1,0:T(8,128)(2,1)} %broadcast_in_dim.57), calls=%async_computation.10 | async-start | bytes 1179648 | tf_op jit(solution)/shard_map/all_to_all | solution.py:38
  146.9 68.3 %collective-permute-start.5 = (bf16[256,768]{1,0:T(8,128)(2,1)}, bf16[256,768]{1,0:T(8,128)(2,1)}, u32[]{:S(2)}, u32[]{:S(2)}) collective-permute-start(bf16[256,768]{1,0:T(8,128)(2,1)} %convolution_convert_fusion.2), channel_id=1, source_target_pairs={{0,4},{4,0},{8,12},{12,8},{16,20},{20,16},{24,28},{28,24},{1,5},{5... | collective-permute-start | bytes 1179656 | tf_op jit(solution)/shard_map/ppermute | solution.py:35
  161.4 18.9 %all-to-all-start.11 = ((bf16[4,96,768]{2,1,0:T(8,128)(2,1)}), bf16[4,96,768]{2,1,0:T(8,128)(2,1)S(1)}, u32[]{:S(2)}, u32[]{:S(2)}) async-start(bf16[4,96,768]{2,1,0:T(8,128)(2,1)} %broadcast_in_dim.58), calls=%async_computation.11 | async-start | bytes 1179648 | tf_op jit(solution)/shard_map/all_to_all | solution.py:38
  180.3 15.4 %all-to-all-start.5 = ((bf16[4,96,512]{2,1,0:T(8,128)(2,1)}), bf16[4,96,512]{2,1,0:T(8,128)(2,1)}, u32[]{:S(2)}, u32[]{:S(2)}) async-start(bf16[4,96,512]{2,1,0:T(8,128)(2,1)} %pad_maximum_fusion), calls=%async_computation.5 | async-start | bytes 786432 | tf_op jit(solution)/shard_map/all_to_all | solution.py:38
  184.4 1.6 copy-start.6
  184.4 1.9 copy-start.8
  195.7 15.4 %all-to-all-start.12 = ((bf16[4,96,512]{2,1,0:T(8,128)(2,1)}), bf16[4,96,512]{2,1,0:T(8,128)(2,1)}, u32[]{:S(2)}, u32[]{:S(2)}) async-start(bf16[4,96,512]{2,1,0:T(8,128)(2,1)} %pad_maximum_fusion.1), calls=%async_computation.12 | async-start | bytes 786432 | tf_op jit(solution)/shard_map/all_to_all | solution.py:38
  201.0 16.7 %collective-permute-start.4 = (bf16[256,768]{1,0:T(8,128)(2,1)}, bf16[256,768]{1,0:T(8,128)(2,1)}, u32[]{:S(2)}, u32[]{:S(2)}) collective-permute-start(bf16[256,768]{1,0:T(8,128)(2,1)} %convolution_convert_fusion.3), channel_id=1, source_target_pairs={{0,4},{4,0},{8,12},{12,8},{16,20},{20,16},{24,28},{28,24},{1,5},{5... | collective-permute-start | bytes 1179656 | tf_op jit(solution)/shard_map/ppermute | solution.py:35
  203.7 23.4 %collective-permute-start.3 = (bf16[256,768]{1,0:T(8,128)(2,1)}, bf16[256,768]{1,0:T(8,128)(2,1)}, u32[]{:S(2)}, u32[]{:S(2)}) collective-permute-start(bf16[256,768]{1,0:T(8,128)(2,1)} %convolution_convert_fusion.4), channel_id=1, source_target_pairs={{0,4},{4,0},{8,12},{12,8},{16,20},{20,16},{24,28},{28,24},{1,5},{5... | collective-permute-start | bytes 1179656 | tf_op jit(solution)/shard_map/ppermute | solution.py:35
  211.1 11.6 %all-to-all-start.6 = ((bf16[96,4,512]{2,1,0:T(4,128)(2,1)}), bf16[96,4,512]{2,1,0:T(4,128)(2,1)}, u32[]{:S(2)}, u32[]{:S(2)}) async-start(bf16[96,4,512]{2,1,0:T(4,128)(2,1)} %copy.44), calls=%async_computation.6 | async-start | bytes 786432 | tf_op jit(solution)/shard_map/all_to_all | solution.py:43
  222.0 6.5 %copy-start.3 = (f32[256,1,768]{2,0,1:T(8,128)S(1)}, f32[256,1,768]{2,0,1:T(8,128)}, u32[]{:S(2)}) copy-start(f32[256,1,768]{2,0,1:T(8,128)} %add_bitcast_fusion) | copy-start | bytes 2359300
  222.7 13.0 %all-to-all-start.13 = ((bf16[96,4,512]{2,1,0:T(4,128)(2,1)}), bf16[96,4,512]{2,1,0:T(4,128)(2,1)}, u32[]{:S(2)}, u32[]{:S(2)}) async-start(bf16[96,4,512]{2,1,0:T(4,128)(2,1)} %copy.46), calls=%async_computation.13 | async-start | bytes 786432 | tf_op jit(solution)/shard_map/all_to_all | solution.py:43
  227.0 1.5 copy-start.4
  239.4 3.1 %copy-start.10 = (pred[384,96]{0,1:T(8,128)(4,1)S(1)}, pred[384,96]{0,1:T(8,128)(4,1)}, u32[]{:S(2)}) copy-start(pred[384,96]{0,1:T(8,128)(4,1)} %copy-done.9) | copy-start | bytes 110596
  244.9 2.6 %copy-start.11 = (pred[384,4,24]{0,2,1:T(8,128)(4,1)S(1)}, pred[384,4,24]{0,2,1:T(8,128)(4,1)}, u32[]{:S(2)}) copy-start(pred[384,4,24]{0,2,1:T(8,128)(4,1)} %fusion.18) | copy-start | bytes 110596
  247.2 2.1 copy-start.13
  247.2 2.1 copy-start.14
  (2 other events, 1.5 us)

commit v2 on v0

v2 whole, which is shorter than its diff:
```python
import functools

import jax
import jax.numpy as jnp
from jax import lax
from jax.experimental import pallas as pl
from jax.experimental.pallas import tpu as pltpu
from jax.sharding import PartitionSpec as P

CAP = 24
F32 = jnp.float32
BF16 = jnp.bfloat16
VMEM = pl.BlockSpec(memory_space=pltpu.VMEM)
SMEM = pl.BlockSpec(memory_space=pltpu.SMEM)


def dot(a, b, ca, cb):
    return lax.dot_general(a, b, (((ca,), (cb,)), ((), ())), preferred_element_type=F32)


def shape(dims, dtype=BF16):
    return jax.ShapeDtypeStruct(tuple(dims), dtype)


def call(kernel, name, outs, args, flops=0, scratch=(), n_smem=0):
    moved = sum(a.size * a.dtype.itemsize for a in list(args) + list(outs))
    return pl.pallas_call(
        kernel,
        name=name,
        out_shape=list(outs),
        in_specs=[SMEM] * n_smem + [VMEM] * (len(args) - n_smem),
        out_specs=[VMEM] * len(outs),
        scratch_shapes=list(scratch),
        cost_estimate=pl.CostEstimate(
            flops=int(flops), bytes_accessed=int(moved), transcendentals=0
        ),
    )(*args)


def flip_if(odd, x, d_own):
    flipped = jnp.concatenate([x[:, d_own:], x[:, :d_own]], axis=1)
    return jnp.where(odd, flipped, x)


def scatter_kernel(n_ep, n_hi, d_own, place, ids, codes, tokens, grads, *outs):
    sends, onehot_ref, weight_ref = outs[:n_ep], outs[n_ep], outs[n_ep + 1]
    hi, low, ep = place[0], place[1], place[2]
    n_tok = tokens.shape[0]
    span = 2 * d_own
    members, weights = [], []
    for j in range(n_ep):
        hit = ids[...] == (ep ^ j)
        members.append(jnp.max(jnp.where(hit, 1.0, 0.0), axis=0, keepdims=True))
        code = jnp.sum(jnp.where(hit, codes[...], 0), axis=0, keepdims=True)
        weights.append(code.astype(F32) / 65536.0)
    pad = [jnp.zeros((1, n_tok), F32)] * (-n_ep % 8)
    member = jnp.concatenate(members + pad, axis=0)
    before = lax.broadcasted_iota(jnp.int32, (n_tok, n_tok), 0)
    after = lax.broadcasted_iota(jnp.int32, (n_tok, n_tok), 1)
    upper = jnp.where(before <= after, 1.0, 0.0).astype(BF16)
    count = dot(member.astype(BF16), upper, 1, 0)
    slot = lax.broadcasted_iota(jnp.int32, (CAP, n_tok), 0).astype(F32) + 1.0
    for j in range(n_ep):
        placed = (slot == count[j : j + 1]) & (members[j] > 0.5)
        rows = pl.ds(j * CAP, CAP)
        onehot_ref[rows, :] = jnp.where(placed, 1.0, 0.0).astype(BF16)
        weight_ref[rows, :] = jnp.sum(jnp.where(placed, weights[j], 0.0), axis=1, keepdims=True)
    onehot = onehot_ref[...]
    weight = weight_ref[...]
    odd = low == 1
    for k in range(n_hi):
        cols = pl.ds(pl.multiple_of((hi ^ k) * span, span), span)
        x = flip_if(odd, dot(onehot, tokens[:, cols], 1, 0), d_own)
        g = flip_if(odd, dot(onehot, grads[:, cols], 1, 0) * weight, d_own)
        for j in range(n_ep):
            rows = slice(j * CAP, (j + 1) * CAP)
            sends[j][k, 0] = x[rows].astype(BF16)
            sends[j][k, 1] = g[rows].astype(BF16)


def repack_kernel(n_in, *refs):
    ins, outs = refs[:n_in], refs[n_in:]
    for k, out in enumerate(outs):
        for i, ref in enumerate(ins):
            out[:, i * CAP : (i + 1) * CAP, :] = ref[k]


def unpack_kernel(n_in, *refs):
    ins, outs = refs[:n_in], refs[n_in:]
    for k, ref in enumerate(ins):
        for i, out in enumerate(outs):
            out[k] = ref[:, i * CAP : (i + 1) * CAP, :]


def partial_kernel(n_hi, *refs):
    slots, own, peer, outs = refs[:n_hi], refs[n_hi], refs[n_hi + 1], refs[n_hi + 2 :]
    rows, d_own, ff = slots[0].shape[1], own.shape[1], own.shape[2]
    x = jnp.concatenate([s[0] for s in slots], axis=0)
    g = jnp.concatenate([s[1] for s in slots], axis=0)
    for m, a in enumerate((x, x, g)):
        part = dot(a[:, :d_own], own[m], 1, 0) + dot(a[:, d_own:], peer[m], 1, 0)
        for k in range(n_hi):
            block = part[k * rows : (k + 1) * rows]
            outs[k][:, m * ff : (m + 1) * ff] = block.astype(outs[k].dtype)


def add_kernel(a, b, out):
    out[...] = (a[...] + b[...].astype(F32)).astype(out.dtype)


def act_kernel(n_in, *refs):
    ins, out = refs[:n_in], refs[n_in]
    ff = out.shape[1] // 3

    def total(m):
        cols = slice(m * ff, (m + 1) * ff)
        t = ins[0][:, cols]
        for ref in ins[1:]:
            t = t + ref[:, cols].astype(F32)
        return t

    pre_gate, pre_up, hidden_grad = total(0), total(1), total(2)
    soft = jax.nn.sigmoid(pre_gate)
    active = pre_gate * soft
    out[:, :ff] = (active * pre_up).astype(BF16)
    out[:, ff : 2 * ff] = (
        hidden_grad * pre_up * soft * (1.0 + pre_gate * (1.0 - soft))
    ).astype(BF16)
    out[:, 2 * ff :] = (hidden_grad * active).astype(BF16)


def back_kernel(n_hi, *refs):
    acts, own, peer, outs = refs[:n_hi], refs[n_hi], refs[n_hi + 1], refs[n_hi + 2 :]
    rows, d_own, ff = acts[0].shape[0], own.shape[1], own.shape[2]

    def part(m):
        return jnp.concatenate([a[:, m * ff : (m + 1) * ff] for a in acts], axis=0)

    hidden, gate, up = part(0), part(1), part(2)
    for i, w in enumerate((own, peer)):
        cols = slice(i * d_own, (i + 1) * d_own)
        out = dot(hidden, w[2], 1, 1).astype(BF16)
        grad = (dot(gate, w[0], 1, 1) + dot(up, w[1], 1, 1)).astype(BF16)
        for k in range(n_hi):
            outs[k][0, :, cols] = out[k * rows : (k + 1) * rows]
            outs[k][1, :, cols] = grad[k * rows : (k + 1) * rows]


def weight_kernel(n_in, *refs):
    slots, acts, own, peer = refs[:n_in], refs[n_in : 2 * n_in], refs[-2], refs[-1]
    d_own, ff = own.shape[1], own.shape[2]
    x = jnp.concatenate([s[0] for s in slots], axis=0)
    g = jnp.concatenate([s[1] for s in slots], axis=0)

    def part(m):
        return jnp.concatenate([a[:, m * ff : (m + 1) * ff] for a in acts], axis=0)

    for m, (a, h) in enumerate(((x, 1), (x, 2), (g, 0))):
        both = dot(a, part(h), 0, 0)
        own[m] = both[:d_own]
        peer[m] = both[d_own:].astype(BF16)


def combine_kernel(n_ep, n_hi, d_own, place, onehot_ref, weight_ref, *refs):
    backs, moe, grad = refs[:n_ep], refs[n_ep], refs[n_ep + 1]
    hi, odd = place[0], place[1] == 1
    span = 2 * d_own
    onehot, weight = onehot_ref[...], weight_ref[...]
    thrice = jnp.concatenate([onehot] * 3, axis=0)
    for k in range(n_hi):
        cols = pl.ds(pl.multiple_of((hi ^ k) * span, span), span)
        out = jnp.concatenate([b[k, 0].astype(F32) for b in backs], axis=0) * weight
        first = out.astype(BF16)
        rest = out - first.astype(F32)
        second = rest.astype(BF16)
        third = (rest - second.astype(F32)).astype(BF16)
        terms = jnp.concatenate([first, second, third], axis=0)
        moe[:, cols] = flip_if(odd, dot(thrice, terms, 0, 0), d_own).astype(BF16)
        back = jnp.concatenate([b[k, 1].astype(F32) for b in backs], axis=0).astype(BF16)
        grad[:, cols] = flip_if(odd, dot(onehot, back, 0, 0), d_own).astype(BF16)


def body(tokens, expert_ids, gate_codes, out_grad, expert_weights):
    n_ep = lax.axis_size("ep")
    n_ctx = lax.axis_size("ctx")
    n_hi = n_ctx // 2
    n_tok, width = tokens.shape
    d_own, _, _, ff = expert_weights.shape
    span = 2 * d_own
    ctx = lax.axis_index("ctx")
    place = jnp.stack([ctx // 2, ctx % 2, lax.axis_index("ep")]).astype(jnp.int32)
    bits = [1 << b for b in range(n_hi.bit_length() - 1)]

    def over_ctx(x, flip):
        return lax.ppermute(x, "ctx", [(c, c ^ flip) for c in range(n_ctx)])

    def over_line(x, k):
        return over_ctx(x, 2 * k)

    def over_ep(x, j):
        return lax.ppermute(x, "ep", [(e, e ^ j) for e in range(n_ep)])

    own = jnp.transpose(expert_weights[:, 0], (1, 0, 2))
    peer = over_ctx(own, 1)

    send = (n_hi, 2, CAP, span)
    slots_flops = 4 * n_ep * CAP * n_tok * width
    *sends, onehot, weight = call(
        functools.partial(scatter_kernel, n_ep, n_hi, d_own),
        "scatter",
        [shape(send)] * n_ep + [shape((n_ep * CAP, n_tok)), shape((n_ep * CAP, 1), F32)],
        (place, expert_ids.T, gate_codes.T, tokens, out_grad),
        flops=slots_flops,
        n_smem=1,
    )
    half = max(n_ep // 2, 1)
    groups = [list(range(g, g + half)) for g in range(0, n_ep, half)]
    taken = [sends[0]] + [over_ep(sends[j], j) for j in range(1, n_ep)]
    rows = half * CAP
    mat_flops = 2 * n_hi * rows * span * ff

    slots = []
    for group in groups:
        packed = call(
            functools.partial(repack_kernel, half),
            "repack",
            [shape((2, rows, span))] * n_hi,
            [taken[j] for j in group],
        )
        slots.append([packed[0]] + [over_line(packed[k], k) for k in range(1, n_hi)])

    parts = []
    for g in range(len(groups)):
        parts.append(
            call(
                functools.partial(partial_kernel, n_hi),
                "partial",
                [shape((rows, 3 * ff), F32 if k % 2 == 0 else BF16) for k in range(n_hi)],
                (*slots[g], own, peer),
                flops=3 * mat_flops,
            )
        )

    acts = []
    for g in range(len(groups)):
        chunk = list(parts[g])
        last = [chunk[0]]
        for bit in bits:
            sent = [k for k in range(bit, n_hi, 2 * bit)]
            moved = {k: over_line(chunk[k], bit) for k in sent[::-1]}
            for k in sent[::-1]:
                if k == bit:
                    last.append(moved[k])
                else:
                    into = k ^ bit
                    dtype = BF16 if into & (2 * bit) else F32
                    (chunk[into],) = call(
                        add_kernel, "add", [shape((rows, 3 * ff), dtype)], (chunk[into], moved[k])
                    )
        (act,) = call(
            functools.partial(act_kernel, len(last)), "act", [shape((rows, 3 * ff))], last
        )
        held = {0: act}
        for bit in bits[::-1]:
            for k in list(held):
                held[k ^ bit] = over_line(held[k], bit)
        acts.append([held[k] for k in range(n_hi)])

    returns = []
    for g in range(len(groups)):
        backs = call(
            functools.partial(back_kernel, n_hi),
            "back",
            [shape((2, rows, span))] * n_hi,
            (*acts[g], own, peer),
            flops=3 * mat_flops,
        )
        returns.append([backs[0]] + [over_line(backs[k], k) for k in range(1, n_hi)])

    all_slots = sum(slots, [])
    all_acts = sum(acts, [])
    own_grad, peer_grad = call(
        functools.partial(weight_kernel, len(all_slots)),
        "weight",
        [shape((3, d_own, ff), F32), shape((3, d_own, ff))],
        (*all_slots, *all_acts),
        flops=6 * mat_flops,
    )
    peer_grad = over_ctx(peer_grad, 1)
    weight_grads = jnp.transpose(own_grad + peer_grad.astype(F32), (1, 0, 2))[:, None]

    backs = []
    for g, group in enumerate(groups):
        unpacked = call(
            functools.partial(unpack_kernel, n_hi), "unpack", [shape(send)] * half, returns[g]
        )
        backs += [x if j == 0 else over_ep(x, j) for j, x in zip(group, unpacked)]
    moe_out, input_grad = call(
        functools.partial(combine_kernel, n_ep, n_hi, d_own),
        "combine",
        [shape((n_tok, width))] * 2,
        (place, onehot, weight, *backs),
        flops=2 * slots_flops,
        n_smem=1,
    )
    return moe_out, input_grad, weight_grads


def solution(mesh):
    by_token = P(("ctx", "ep"), None)
    by_weight = P("ctx", "ep", None, None)
    return jax.shard_map(
        body,
        mesh=mesh,
        in_specs=(by_token, by_token, by_token, by_token, by_weight),
        out_specs=(by_token, by_token, by_weight),
        check_vma=False,
    )
```

time: 340 us -> 151 us (0.44)
  waiting for transfers between devices: 266 us -> 59.1 us
  Pallas kernels: 0 us -> 42.1 us
  matrix products: 29.5 us -> 0 us
  starting transfers between devices: 14.8 us -> 35.9 us
  between operations: 14.2 us -> 0.81 us
  other arithmetic: 8.13 us -> 0.82 us
  local copies, waits for them, and re-layouts: 6.59 us -> 10.4 us
    reduce_scatter x1 -> x0, waiting for transfers between devices: 128 us -> none  [body(): lax.psum_scatter(full_terms.astype(jnp.bfloat16), 'ctx', scatter_dimensio...]
    all_gather x1 -> x0, waiting for transfers between devices: 122 us -> none  [body(): gathered = lax.all_gather(expert_weights, 'ctx', axis=0, tiled=True)]
    ppermute x0 -> x32, waiting for transfers between devices: none -> 59.1 us  [the longest x26 48.6 us: over_ctx(): return lax.ppermute(x, 'ctx', [(c, c ^ flip) for c in range(n_ctx)])]
    pallas_call x0 -> x15, Pallas kernels: none -> 42.1 us  [call(): pl.pallas_call(kernel, name=name, out_shape=list(outs), in_specs=[SMEM] *...]
    ppermute x0 -> x32, starting transfers between devices: none -> 35.9 us  [the longest x26 33.7 us: over_ctx(): return lax.ppermute(x, 'ctx', [(c, c ^ flip) for c in range(n_ctx)])]
    dot_general x16 -> x0, matrix products: 29.5 us -> none  [the longest x4 4.25 us: body(): jnp.dot(onehot[:, expert, :], out_back[expert], preferred_element_type=jn...]
    all_to_all x4 -> x0, waiting for transfers between devices: 15.5 us -> none  [the longest x1 6.24 us: body(): lax.all_to_all(send_grad, 'ep', split_axis=0, concat_axis=0, tiled=True)]
    all_to_all x4 -> x0, starting transfers between devices: 14.7 us -> none  [the longest x1 4.23 us: body(): lax.all_to_all(send_grad, 'ep', split_axis=0, concat_axis=0, tiled=True)]
  transfers between devices with their start and end apart: 6 -> 32, of which waited for: 5 -> 15; matrix products, arithmetic and copies ran while one was open for 8% -> 0% of each run, Pallas kernels for 0% -> 25%
where the time goes in v2:
time: 151 us; the launch traced here: 149 us
  waiting for transfers between devices  59.1 us (39%)
  Pallas kernels  42.1 us (28%)
  starting transfers between devices  35.9 us (24%)
  local copies, waits for them, and re-layouts  10.4 us (7%)
    ppermute x26, waiting for transfers between devices, over_ctx(): return lax.ppermute(x, 'ctx', [(c, c ^ flip) for c in range(n_ctx)])  48.6 us
    pallas_call x15, Pallas kernels, call(): pl.pallas_call(kernel, name=name, out_shape=list(outs), in_specs=[SMEM] *...  42.1 us
    ppermute x26, starting transfers between devices, over_ctx(): return lax.ppermute(x, 'ctx', [(c, c ^ flip) for c in range(n_ctx)])  33.7 us
    ppermute x6, waiting for transfers between devices, over_ep(): return lax.ppermute(x, 'ep', [(e, e ^ j) for e in range(n_ep)])  10.5 us
    unnamed x49, local copies, waits for them, and re-layouts  10.4 us
  transfers between devices with their start and end apart: 32, of which 15 were waited for; matrix products, arithmetic and copies ran while one was open for 0% of the time, Pallas kernels for 25%

profile of v2, /device:TPU:0, one launch (start us, length us, event | category | flops | bytes accessed | tf_op | source)
XLA Modules:
  0.0 149.2 jit_solution(10828205758007026300)
XLA Ops:
  0.6 3.1 %collective-permute-start.4 = (bf16[3,256,768]{2,1,0:T(8,128)(2,1)}, bf16[3,256,768]{2,1,0:T(8,128)(2,1)S(1)}, u32[]{:S(2)}, u32[]{:S(2)}) collective-permute-start(bf16[3,256,768]{2,1,0:T(8,128)(2,1)} %bitcast.12), channel_id=1, source_target_pairs={{0,4},{4,0},{8,12},{12,8},{16,20},{20,16},{24,28},{28,24},{1,5},{5... | collective-permute-start | bytes 3538952 | tf_op jit(solution)/shard_map/ppermute | solution.py:195
  4.3 3.7 %scatter.1 = (bf16[4,2,24,512]{3,2,1,0:T(8,128)(2,1)}, bf16[4,2,24,512]{3,2,1,0:T(8,128)(2,1)}, bf16[4,2,24,512]{3,2,1,0:T(8,128)(2,1)}, bf16[4,2,24,512]{3,2,1,...) custom-call(s32[3]{0:T(128)} %pad_add_fusion.place, s32[8,384]{1,0:T(8,128)} %bitcast.17, s32[8,384]{1,0:T(8,128)} %bitcast.18, ...), custom_call_target="tpu_custom_call" | custom-call | flops 301989888 | bytes 4030860 | tf_op jit(solution)/shard_map/scatter/pallas_call | solution.py:27
  10.1 5.8 %collective-permute-done.15.refs_0_ = bf16[4,2,24,512]{3,2,1,0:T(8,128)(2,1)S(1)} collective-permute-done((bf16[4,2,24,512]{3,2,1,0:T(8,128)(2,1)}, bf16[4,2,24,512]{3,2,1,0:T(8,128)(2,1)S(1)}, u32[]{:S(2)}, u32[]{:S(2)}) %collective-permute-start.15) | collective-permute-done | bytes 196640 | tf_op jit(solution)/shard_map/ppermute | solution.py:201
  15.9 1.9 %collective-permute-done.16.refs_1_ = bf16[4,2,24,512]{3,2,1,0:T(8,128)(2,1)S(1)} collective-permute-done((bf16[4,2,24,512]{3,2,1,0:T(8,128)(2,1)}, bf16[4,2,24,512]{3,2,1,0:T(8,128)(2,1)S(1)}, u32[]{:S(2)}, u32[]{:S(2)}) %collective-permute-start.16) | collective-permute-done | bytes 196640 | tf_op jit(solution)/shard_map/ppermute | solution.py:201
  18.5 1.8 %repack.3 = (bf16[2,48,512]{2,1,0:T(8,128)(2,1)}, bf16[2,48,512]{2,1,0:T(8,128)(2,1)}, bf16[2,48,512]{2,1,0:T(8,128)(2,1)}, bf16[2,48,512]{2,1,0:T(8,128)(2,1)}) custom-call(bf16[4,2,24,512]{3,2,1,0:T(8,128)(2,1)} %copy-done.15, bf16[4,2,24,512]{3,2,1,0:T(8,128)(2,1)} %copy-done.16), custom_call_target="tpu_custom_call" | custom-call | bytes 786432 | tf_op jit(solution)/shard_map/repack/pallas_call | solution.py:27
  21.9 2.6 %collective-permute-start.18 = (bf16[2,48,512]{2,1,0:T(8,128)(2,1)}, bf16[2,48,512]{2,1,0:T(8,128)(2,1)S(1)}, u32[]{:S(2)}, u32[]{:S(2)}) collective-permute-start(bf16[2,48,512]{2,1,0:T(8,128)(2,1)} %get-tuple-element.63), channel_id=1, source_target_pairs={{0,16},{4,20},{8,24},{12,28},{16,0},{20,4},{24,8},{28,12},{1,17},{... | collective-permute-start | bytes 294920 | tf_op jit(solution)/shard_map/ppermute | solution.py:195
  27.9 3.5 %collective-permute-start.2 = (bf16[2,48,512]{2,1,0:T(8,128)(2,1)}, bf16[2,48,512]{2,1,0:T(8,128)(2,1)S(1)}, u32[]{:S(2)}, u32[]{:S(2)}) collective-permute-start(bf16[2,48,512]{2,1,0:T(8,128)(2,1)} %get-tuple-element.47), channel_id=1, source_target_pairs={{0,16},{4,20},{8,24},{12,28},{16,0},{20,4},{24,8},{28,12},{1,17},{... | collective-permute-start | bytes 294920 | tf_op jit(solution)/shard_map/ppermute | solution.py:195
  33.0 2.5 %collective-permute-start.3 = (bf16[2,48,512]{2,1,0:T(8,128)(2,1)}, bf16[2,48,512]{2,1,0:T(8,128)(2,1)S(1)}, u32[]{:S(2)}, u32[]{:S(2)}) collective-permute-start(bf16[2,48,512]{2,1,0:T(8,128)(2,1)} %get-tuple-element.48), channel_id=1, source_target_pairs={{0,24},{4,28},{8,16},{12,20},{16,8},{20,12},{24,0},{28,4},{1,25},{... | collective-permute-start | bytes 294920 | tf_op jit(solution)/shard_map/ppermute | solution.py:195
  36.5 3.5 %partial.3 = (f32[48,2304]{1,0:T(8,128)}, bf16[48,2304]{1,0:T(8,128)(2,1)}, f32[48,2304]{1,0:T(8,128)}, bf16[48,2304]{1,0:T(8,128)(2,1)}) custom-call(bf16[2,48,512]{2,1,0:T(8,128)(2,1)} %get-tuple-element.61.refs_0_.refs_4_, bf16[2,48,512]{2,1,0:T(8,128)(2,1)} %copy-done.17, bf16[2,48,512]{2,1,0:T(8,128)(2,1)} %copy-done.18, ...), custom_call_target="tpu_custom_call" | custom-call | flops 452984832 | bytes 4079616 | tf_op jit(solution)/shard_map/partial/pallas_call | solution.py:27
  40.0 3.4 %collective-permute-start.21 = (bf16[48,2304]{1,0:T(8,128)(2,1)}, bf16[48,2304]{1,0:T(8,128)(2,1)S(1)}, u32[]{:S(2)}, u32[]{:S(2)}) collective-permute-start(bf16[48,2304]{1,0:T(8,128)(2,1)} %get-tuple-element.68), channel_id=1, source_target_pairs={{0,8},{4,12},{8,0},{12,4},{16,24},{20,28},{24,16},{28,20},{1,9},{5... | collective-permute-start | bytes 663560 | tf_op jit(solution)/shard_map/ppermute | solution.py:195
  44.1 3.5 %partial.2 = (f32[48,2304]{1,0:T(8,128)}, bf16[48,2304]{1,0:T(8,128)(2,1)}, f32[48,2304]{1,0:T(8,128)}, bf16[48,2304]{1,0:T(8,128)(2,1)}) custom-call(bf16[2,48,512]{2,1,0:T(8,128)(2,1)} %get-tuple-element.45.refs_0_, bf16[2,48,512]{2,1,0:T(8,128)(2,1)} %copy-done.20, bf16[2,48,512]{2,1,0:T(8,128)(2,1)} %copy-done.21, bf16[2,48,512]{2,1,0:T(8,128)(2,1)} %copy-done.22, ...), custom_call_target="tpu_custom_call" | custom-call | flops 452984832 | bytes 4079616 | tf_op jit(solution)/shard_map/partial/pallas_call | solution.py:27
  54.1 8.3 %collective-permute-done.6.b = bf16[48,2304]{1,0:T(8,128)(2,1)S(1)} collective-permute-done((bf16[48,2304]{1,0:T(8,128)(2,1)}, bf16[48,2304]{1,0:T(8,128)(2,1)S(1)}, u32[]{:S(2)}, u32[]{:S(2)}) %collective-permute-start.6) | collective-permute-done | bytes 221216 | tf_op jit(solution)/shard_map/ppermute | solution.py:195
  64.8 3.0 %collective-permute-done.20.refs_1_ = bf16[48,2304]{1,0:T(8,128)(2,1)S(1)} collective-permute-done((bf16[48,2304]{1,0:T(8,128)(2,1)S(1)}, bf16[48,2304]{1,0:T(8,128)(2,1)S(1)}, u32[]{:S(2)}, u32[]{:S(2)}) %collective-permute-start.20) | collective-permute-done | bytes 221216 | tf_op jit(solution)/shard_map/ppermute | solution.py:195
  68.6 2.0 %act.3.refs_0_.refs_12_ = bf16[48,2304]{1,0:T(8,128)(2,1)} custom-call(f32[48,2304]{1,0:T(8,128)} %get-tuple-element.65.refs_0_, bf16[48,2304]{1,0:T(8,128)(2,1)} %copy-done.11, bf16[48,2304]{1,0:T(8,128)(2,1)} %copy-done.13), custom_call_target="tpu_custom_call" | custom-call | bytes 1105920 | tf_op jit(solution)/shard_map/act/pallas_call | solution.py:27
  71.6 14.3 %collective-permute-done.7.refs_2_ = bf16[48,2304]{1,0:T(8,128)(2,1)S(1)} collective-permute-done((bf16[48,2304]{1,0:T(8,128)(2,1)}, bf16[48,2304]{1,0:T(8,128)(2,1)S(1)}, u32[]{:S(2)}, u32[]{:S(2)}) %collective-permute-start.7) | collective-permute-done | bytes 221216 | tf_op jit(solution)/shard_map/ppermute | solution.py:195
  86.6 2.0 %act.2.refs_0_.refs_8_ = bf16[48,2304]{1,0:T(8,128)(2,1)} custom-call(f32[48,2304]{1,0:T(8,128)} %get-tuple-element.49.refs_0_, bf16[48,2304]{1,0:T(8,128)(2,1)} %copy-done.10, bf16[48,2304]{1,0:T(8,128)(2,1)} %copy-done.12), custom_call_target="tpu_custom_call" | custom-call | bytes 1105920 | tf_op jit(solution)/shard_map/act/pallas_call | solution.py:27
  91.6 4.6 %collective-permute-done.9.refs_2_.refs_10_ = bf16[48,2304]{1,0:T(8,128)(2,1)S(1)} collective-permute-done((bf16[48,2304]{1,0:T(8,128)(2,1)}, bf16[48,2304]{1,0:T(8,128)(2,1)S(1)}, u32[]{:S(2)}, u32[]{:S(2)}) %collective-permute-start.9) | collective-permute-done | bytes 221216 | tf_op jit(solution)/shard_map/ppermute | solution.py:195
  96.3 3.2 %collective-permute-done.23.refs_1_.refs_13_ = bf16[48,2304]{1,0:T(8,128)(2,1)S(1)} collective-permute-done((bf16[48,2304]{1,0:T(8,128)(2,1)}, bf16[48,2304]{1,0:T(8,128)(2,1)S(1)}, u32[]{:S(2)}, u32[]{:S(2)}) %collective-permute-start.23) | collective-permute-done | bytes 221216 | tf_op jit(solution)/shard_map/ppermute | solution.py:195
  99.5 4.7 %collective-permute-done.8.refs_1_.refs_9_ = bf16[48,2304]{1,0:T(8,128)(2,1)S(1)} collective-permute-done((bf16[48,2304]{1,0:T(8,128)(2,1)}, bf16[48,2304]{1,0:T(8,128)(2,1)S(1)}, u32[]{:S(2)}, u32[]{:S(2)}) %collective-permute-start.8) | collective-permute-done | bytes 221216 | tf_op jit(solution)/shard_map/ppermute | solution.py:195
  104.2 2.4 %collective-permute-done.25.refs_3_.refs_15_ = bf16[48,2304]{1,0:T(8,128)(2,1)S(1)} collective-permute-done((bf16[48,2304]{1,0:T(8,128)(2,1)S(1)}, bf16[48,2304]{1,0:T(8,128)(2,1)S(1)}, u32[]{:S(2)}, u32[]{:S(2)}) %collective-permute-start.25) | collective-permute-done | bytes 221216 | tf_op jit(solution)/shard_map/ppermute | solution.py:195
  106.6 2.4 %collective-permute-done.10.refs_3_.refs_11_ = bf16[48,2304]{1,0:T(8,128)(2,1)S(1)} collective-permute-done((bf16[48,2304]{1,0:T(8,128)(2,1)S(1)}, bf16[48,2304]{1,0:T(8,128)(2,1)S(1)}, u32[]{:S(2)}, u32[]{:S(2)}) %collective-permute-start.10) | collective-permute-done | bytes 221216 | tf_op jit(solution)/shard_map/ppermute | solution.py:195
  109.7 5.0 %weight.1 = (f32[3,256,768]{2,1,0:T(8,128)}, bf16[3,256,768]{2,1,0:T(8,128)(2,1)}) custom-call(bf16[2,48,512]{2,1,0:T(8,128)(2,1)} %get-tuple-element.45.refs_0_, bf16[2,48,512]{2,1,0:T(8,128)(2,1)} %copy-done.20, bf16[2,48,512]{2,1,0:T(8,128)(2,1)} %copy-done.21, bf16[2,48,512]{2,1,0:T(8,128)(2,1)} %copy-done.22, ...), custom_call_target="tpu_custom_call" | custom-call | flops 905969664 | bytes 6094848 | tf_op jit(solution)/shard_map/weight/pallas_call | solution.py:27
  115.1 3.6 %back.3 = (bf16[2,48,512]{2,1,0:T(8,128)(2,1)}, bf16[2,48,512]{2,1,0:T(8,128)(2,1)}, bf16[2,48,512]{2,1,0:T(8,128)(2,1)}, bf16[2,48,512]{2,1,0:T(8,128)(2,1)}) custom-call(bf16[48,2304]{1,0:T(8,128)(2,1)} %act.3.refs_0_.refs_12_, bf16[48,2304]{1,0:T(8,128)(2,1)} %copy-done.6, bf16[48,2304]{1,0:T(8,128)(2,1)} %copy-done.3, bf16[48,2304]{1,0:T(8,128)(2,1)} %copy-done.7, ...), custom_call_target="tpu_custom_call" | custom-call | flops 452984832 | bytes 3637248 | tf_op jit(solution)/shard_map/back/pallas_call | solution.py:27
  118.8 2.5 %collective-permute-start.27 = (bf16[2,48,512]{2,1,0:T(8,128)(2,1)}, bf16[2,48,512]{2,1,0:T(8,128)(2,1)}, u32[]{:S(2)}, u32[]{:S(2)}) collective-permute-start(bf16[2,48,512]{2,1,0:T(8,128)(2,1)} %get-tuple-element.71), channel_id=1, source_target_pairs={{0,16},{4,20},{8,24},{12,28},{16,0},{20,4},{24,8},{28,12},{1,17},{... | collective-permute-start | bytes 294920 | tf_op jit(solution)/shard_map/ppermute | solution.py:195
  121.3 1.8 %collective-permute-start.28 = (bf16[2,48,512]{2,1,0:T(8,128)(2,1)}, bf16[2,48,512]{2,1,0:T(8,128)(2,1)}, u32[]{:S(2)}, u32[]{:S(2)}) collective-permute-start(bf16[2,48,512]{2,1,0:T(8,128)(2,1)} %get-tuple-element.72), channel_id=1, source_target_pairs={{0,24},{4,28},{8,16},{12,20},{16,8},{20,12},{24,0},{28,4},{1,25},{... | collective-permute-start | bytes 294920 | tf_op jit(solution)/shard_map/ppermute | solution.py:195
  123.1 3.7 %back.2 = (bf16[2,48,512]{2,1,0:T(8,128)(2,1)}, bf16[2,48,512]{2,1,0:T(8,128)(2,1)}, bf16[2,48,512]{2,1,0:T(8,128)(2,1)}, bf16[2,48,512]{2,1,0:T(8,128)(2,1)}) custom-call(bf16[48,2304]{1,0:T(8,128)(2,1)} %act.2.refs_0_.refs_8_, bf16[48,2304]{1,0:T(8,128)(2,1)} %copy-done.4, bf16[48,2304]{1,0:T(8,128)(2,1)} %copy-done.2, bf16[48,2304]{1,0:T(8,128)(2,1)} %copy-done.5, ...), custom_call_target="tpu_custom_call" | custom-call | flops 452984832 | bytes 3637248 | tf_op jit(solution)/shard_map/back/pallas_call | solution.py:27
  126.8 2.5 %collective-permute-start.12 = (bf16[2,48,512]{2,1,0:T(8,128)(2,1)}, bf16[2,48,512]{2,1,0:T(8,128)(2,1)}, u32[]{:S(2)}, u32[]{:S(2)}) collective-permute-start(bf16[2,48,512]{2,1,0:T(8,128)(2,1)} %get-tuple-element.55), channel_id=1, source_target_pairs={{0,16},{4,20},{8,24},{12,28},{16,0},{20,4},{24,8},{28,12},{1,17},{... | collective-permute-start | bytes 294920 | tf_op jit(solution)/shard_map/ppermute | solution.py:195
  129.4 1.8 %collective-permute-start.13 = (bf16[2,48,512]{2,1,0:T(8,128)(2,1)}, bf16[2,48,512]{2,1,0:T(8,128)(2,1)}, u32[]{:S(2)}, u32[]{:S(2)}) collective-permute-start(bf16[2,48,512]{2,1,0:T(8,128)(2,1)} %get-tuple-element.56), channel_id=1, source_target_pairs={{0,24},{4,28},{8,16},{12,20},{16,8},{20,12},{24,0},{28,4},{1,25},{... | collective-permute-start | bytes 294920 | tf_op jit(solution)/shard_map/ppermute | solution.py:195
  133.1 3.1 %collective-permute-done.13.refs_3_ = bf16[2,48,512]{2,1,0:T(8,128)(2,1)} collective-permute-done((bf16[2,48,512]{2,1,0:T(8,128)(2,1)}, bf16[2,48,512]{2,1,0:T(8,128)(2,1)}, u32[]{:S(2)}, u32[]{:S(2)}) %collective-permute-start.13) | collective-permute-done | bytes 98336 | tf_op jit(solution)/shard_map/ppermute | solution.py:195
  138.0 2.6 %collective-permute-done.29.refs_2_ = bf16[4,2,24,512]{3,2,1,0:T(8,128)(2,1)} collective-permute-done((bf16[4,2,24,512]{3,2,1,0:T(8,128)(2,1)}, bf16[4,2,24,512]{3,2,1,0:T(8,128)(2,1)}, u32[]{:S(2)}, u32[]{:S(2)}) %collective-permute-start.29) | collective-permute-done | bytes 196640 | tf_op jit(solution)/shard_map/ppermute | solution.py:201
  140.7 4.4 %combine.1 = (bf16[384,2048]{1,0:T(8,128)(2,1)}, bf16[384,2048]{1,0:T(8,128)(2,1)}) custom-call(s32[3]{0:T(128)} %pad_add_fusion.place, bf16[96,384]{1,0:T(8,128)(2,1)} %get-tuple-element.41.onehot_ref, f32[96,1]{1,0:T(8,128)} %get-tuple-element.42.weight_ref, bf16[4,2,24,512]{3,2,1,0:T(8,128)(2,1)} %get-tuple-element.57.refs_0_, ...), custom_call_target="tpu_custom_call" | custom-call | flops 603979776 | bytes 4006284 | tf_op jit(solution)/shard_map/combine/pallas_call | solution.py:27
  145.3 3.8 %copy.8 = f32[256,1,3,768]{3,1,2,0:T(1,128)} copy(f32[256,1,3,768]{3,0,2,1:T(8,128)S(1)} %add_bitcast_fusion) | data formatting | bytes 4718592
  (98 shorter events, 31.3 us)
Async XLA Ops:
  0.6 34.8 %collective-permute-start.4 = (bf16[3,256,768]{2,1,0:T(8,128)(2,1)}, bf16[3,256,768]{2,1,0:T(8,128)(2,1)S(1)}, u32[]{:S(2)}, u32[]{:S(2)}) collective-permute-start(bf16[3,256,768]{2,1,0:T(8,128)(2,1)} %bitcast.12), channel_id=1, source_target_pairs={{0,4},{4,0},{8,12},{12,8},{16,20},{20,16},{24,28},{28,24},{1,5},{5... | collective-permute-start | bytes 3538952 | tf_op jit(solution)/shard_map/ppermute | solution.py:195
  8.0 8.0 %collective-permute-start.15 = (bf16[4,2,24,512]{3,2,1,0:T(8,128)(2,1)}, bf16[4,2,24,512]{3,2,1,0:T(8,128)(2,1)S(1)}, u32[]{:S(2)}, u32[]{:S(2)}) collective-permute-start(bf16[4,2,24,512]{3,2,1,0:T(8,128)(2,1)} %get-tuple-element.59), channel_id=1, source_target_pairs={{0,2},{1,3},{2,0},{3,1},{4,6},{5,7},{6,4},{7,5},{8,10},{9,11},{10,... | collective-permute-start | bytes 589832 | tf_op jit(solution)/shard_map/ppermute | solution.py:201
  9.5 8.4 %collective-permute-start.16 = (bf16[4,2,24,512]{3,2,1,0:T(8,128)(2,1)}, bf16[4,2,24,512]{3,2,1,0:T(8,128)(2,1)S(1)}, u32[]{:S(2)}, u32[]{:S(2)}) collective-permute-start(bf16[4,2,24,512]{3,2,1,0:T(8,128)(2,1)} %get-tuple-element.60), channel_id=1, source_target_pairs={{0,3},{1,2},{2,1},{3,0},{4,7},{5,6},{6,5},{7,4},{8,11},{9,10},{10,... | collective-permute-start | bytes 589832 | tf_op jit(solution)/shard_map/ppermute | solution.py:201
  9.5 15.3 %collective-permute-start = (bf16[4,2,24,512]{3,2,1,0:T(8,128)(2,1)}, bf16[4,2,24,512]{3,2,1,0:T(8,128)(2,1)S(1)}, u32[]{:S(2)}, u32[]{:S(2)}) collective-permute-start(bf16[4,2,24,512]{3,2,1,0:T(8,128)(2,1)} %get-tuple-element.44), channel_id=1, source_target_pairs={{0,1},{1,0},{2,3},{3,2},{4,5},{5,4},{6,7},{7,6},{8,9},{9,8},{10,11... | collective-permute-start | bytes 589832 | tf_op jit(solution)/shard_map/ppermute | solution.py:201
  20.4 7.5 %collective-permute-start.17 = (bf16[2,48,512]{2,1,0:T(8,128)(2,1)}, bf16[2,48,512]{2,1,0:T(8,128)(2,1)S(1)}, u32[]{:S(2)}, u32[]{:S(2)}) collective-permute-start(bf16[2,48,512]{2,1,0:T(8,128)(2,1)} %get-tuple-element.62), channel_id=1, source_target_pairs={{0,8},{4,12},{8,0},{12,4},{16,24},{20,28},{24,16},{28,20},{1,9},{5... | collective-permute-start | bytes 294920 | tf_op jit(solution)/shard_map/ppermute | solution.py:195
  21.9 11.0 %collective-permute-start.18 = (bf16[2,48,512]{2,1,0:T(8,128)(2,1)}, bf16[2,48,512]{2,1,0:T(8,128)(2,1)S(1)}, u32[]{:S(2)}, u32[]{:S(2)}) collective-permute-start(bf16[2,48,512]{2,1,0:T(8,128)(2,1)} %get-tuple-element.63), channel_id=1, source_target_pairs={{0,16},{4,20},{8,24},{12,28},{16,0},{20,4},{24,8},{28,12},{1,17},{... | collective-permute-start | bytes 294920 | tf_op jit(solution)/shard_map/ppermute | solution.py:195
  24.5 10.9 %collective-permute-start.19 = (bf16[2,48,512]{2,1,0:T(8,128)(2,1)}, bf16[2,48,512]{2,1,0:T(8,128)(2,1)S(1)}, u32[]{:S(2)}, u32[]{:S(2)}) collective-permute-start(bf16[2,48,512]{2,1,0:T(8,128)(2,1)} %get-tuple-element.64), channel_id=1, source_target_pairs={{0,24},{4,28},{8,16},{12,20},{16,8},{20,12},{24,0},{28,4},{1,25},{... | collective-permute-start | bytes 294920 | tf_op jit(solution)/shard_map/ppermute | solution.py:195
  27.2 16.2 %collective-permute-start.1 = (bf16[2,48,512]{2,1,0:T(8,128)(2,1)}, bf16[2,48,512]{2,1,0:T(8,128)(2,1)S(1)}, u32[]{:S(2)}, u32[]{:S(2)}) collective-permute-start(bf16[2,48,512]{2,1,0:T(8,128)(2,1)} %get-tuple-element.46), channel_id=1, source_target_pairs={{0,8},{4,12},{8,0},{12,4},{16,24},{20,28},{24,16},{28,20},{1,9},{5... | collective-permute-start | bytes 294920 | tf_op jit(solution)/shard_map/ppermute | solution.py:195
  27.9 15.5 %collective-permute-start.2 = (bf16[2,48,512]{2,1,0:T(8,128)(2,1)}, bf16[2,48,512]{2,1,0:T(8,128)(2,1)S(1)}, u32[]{:S(2)}, u32[]{:S(2)}) collective-permute-start(bf16[2,48,512]{2,1,0:T(8,128)(2,1)} %get-tuple-element.47), channel_id=1, source_target_pairs={{0,16},{4,20},{8,24},{12,28},{16,0},{20,4},{24,8},{28,12},{1,17},{... | collective-permute-start | bytes 294920 | tf_op jit(solution)/shard_map/ppermute | solution.py:195
  33.0 10.4 %collective-permute-start.3 = (bf16[2,48,512]{2,1,0:T(8,128)(2,1)}, bf16[2,48,512]{2,1,0:T(8,128)(2,1)S(1)}, u32[]{:S(2)}, u32[]{:S(2)}) collective-permute-start(bf16[2,48,512]{2,1,0:T(8,128)(2,1)} %get-tuple-element.48), channel_id=1, source_target_pairs={{0,24},{4,28},{8,16},{12,20},{16,8},{20,12},{24,0},{28,4},{1,25},{... | collective-permute-start | bytes 294920 | tf_op jit(solution)/shard_map/ppermute | solution.py:195
  40.0 9.6 %collective-permute-start.21 = (bf16[48,2304]{1,0:T(8,128)(2,1)}, bf16[48,2304]{1,0:T(8,128)(2,1)S(1)}, u32[]{:S(2)}, u32[]{:S(2)}) collective-permute-start(bf16[48,2304]{1,0:T(8,128)(2,1)} %get-tuple-element.68), channel_id=1, source_target_pairs={{0,8},{4,12},{8,0},{12,4},{16,24},{20,28},{24,16},{28,20},{1,9},{5... | collective-permute-start | bytes 663560 | tf_op jit(solution)/shard_map/ppermute | solution.py:195
  47.6 14.8 %collective-permute-start.6 = (bf16[48,2304]{1,0:T(8,128)(2,1)}, bf16[48,2304]{1,0:T(8,128)(2,1)S(1)}, u32[]{:S(2)}, u32[]{:S(2)}) collective-permute-start(bf16[48,2304]{1,0:T(8,128)(2,1)} %get-tuple-element.52), channel_id=1, source_target_pairs={{0,8},{4,12},{8,0},{12,4},{16,24},{20,28},{24,16},{28,20},{1,9},{5... | collective-permute-start | bytes 663560 | tf_op jit(solution)/shard_map/ppermute | solution.py:195
  48.0 19.9 %collective-permute-start.20 = (bf16[48,2304]{1,0:T(8,128)(2,1)S(1)}, bf16[48,2304]{1,0:T(8,128)(2,1)S(1)}, u32[]{:S(2)}, u32[]{:S(2)}) collective-permute-start(bf16[48,2304]{1,0:T(8,128)(2,1)S(1)} %copy-done.23), channel_id=1, source_target_pairs={{0,8},{4,12},{8,0},{12,4},{16,24},{20,28},{24,16},{28,20},{1,9},{5... | collective-permute-start | bytes 663560 | tf_op jit(solution)/shard_map/ppermute | solution.py:195
  52.1 15.8 %collective-permute-start.22 = (bf16[48,2304]{1,0:T(8,128)(2,1)}, bf16[48,2304]{1,0:T(8,128)(2,1)S(1)}, u32[]{:S(2)}, u32[]{:S(2)}) collective-permute-start(bf16[48,2304]{1,0:T(8,128)(2,1)} %add.18), channel_id=1, source_target_pairs={{0,16},{4,20},{8,24},{12,28},{16,0},{20,4},{24,8},{28,12},{1,17},{... | collective-permute-start | bytes 663560 | tf_op jit(solution)/shard_map/ppermute | solution.py:195
  53.5 18.1 %collective-permute-start.5 = (bf16[48,2304]{1,0:T(8,128)(2,1)}, bf16[48,2304]{1,0:T(8,128)(2,1)S(1)}, u32[]{:S(2)}, u32[]{:S(2)}) collective-permute-start(bf16[48,2304]{1,0:T(8,128)(2,1)} %get-tuple-element.50), channel_id=1, source_target_pairs={{0,8},{4,12},{8,0},{12,4},{16,24},{20,28},{24,16},{28,20},{1,9},{5... | collective-permute-start | bytes 663560 | tf_op jit(solution)/shard_map/ppermute | solution.py:195
  64.8 21.1 %collective-permute-start.7 = (bf16[48,2304]{1,0:T(8,128)(2,1)}, bf16[48,2304]{1,0:T(8,128)(2,1)S(1)}, u32[]{:S(2)}, u32[]{:S(2)}) collective-permute-start(bf16[48,2304]{1,0:T(8,128)(2,1)} %add.17), channel_id=1, source_target_pairs={{0,16},{4,20},{8,24},{12,28},{16,0},{20,4},{24,8},{28,12},{1,17},{... | collective-permute-start | bytes 663560 | tf_op jit(solution)/shard_map/ppermute | solution.py:195
  70.6 20.0 %collective-permute-start.24 = (bf16[48,2304]{1,0:T(8,128)(2,1)}, bf16[48,2304]{1,0:T(8,128)(2,1)S(1)}, u32[]{:S(2)}, u32[]{:S(2)}) collective-permute-start(bf16[48,2304]{1,0:T(8,128)(2,1)} %act.3.refs_0_.refs_12_), channel_id=1, source_target_pairs={{0,16},{4,20},{8,24},{12,28},{16,0},{20,4},{24,8},{28,12},{1,17},{... | collective-permute-start | bytes 663560 | tf_op jit(solution)/shard_map/ppermute | solution.py:195
  88.6 7.6 %collective-permute-start.9 = (bf16[48,2304]{1,0:T(8,128)(2,1)}, bf16[48,2304]{1,0:T(8,128)(2,1)S(1)}, u32[]{:S(2)}, u32[]{:S(2)}) collective-permute-start(bf16[48,2304]{1,0:T(8,128)(2,1)} %act.2.refs_0_.refs_8_), channel_id=1, source_target_pairs={{0,16},{4,20},{8,24},{12,28},{16,0},{20,4},{24,8},{28,12},{1,17},{... | collective-permute-start | bytes 663560 | tf_op jit(solution)/shard_map/ppermute | solution.py:195
  88.6 10.9 %collective-permute-start.23 = (bf16[48,2304]{1,0:T(8,128)(2,1)}, bf16[48,2304]{1,0:T(8,128)(2,1)S(1)}, u32[]{:S(2)}, u32[]{:S(2)}) collective-permute-start(bf16[48,2304]{1,0:T(8,128)(2,1)} %act.3.refs_0_.refs_12_), channel_id=1, source_target_pairs={{0,8},{4,12},{8,0},{12,4},{16,24},{20,28},{24,16},{28,20},{1,9},{5... | collective-permute-start | bytes 663560 | tf_op jit(solution)/shard_map/ppermute | solution.py:195
  89.6 14.6 %collective-permute-start.8 = (bf16[48,2304]{1,0:T(8,128)(2,1)}, bf16[48,2304]{1,0:T(8,128)(2,1)S(1)}, u32[]{:S(2)}, u32[]{:S(2)}) collective-permute-start(bf16[48,2304]{1,0:T(8,128)(2,1)} %act.2.refs_0_.refs_8_), channel_id=1, source_target_pairs={{0,8},{4,12},{8,0},{12,4},{16,24},{20,28},{24,16},{28,20},{1,9},{5... | collective-permute-start | bytes 663560 | tf_op jit(solution)/shard_map/ppermute | solution.py:195
  90.7 15.9 %collective-permute-start.25 = (bf16[48,2304]{1,0:T(8,128)(2,1)S(1)}, bf16[48,2304]{1,0:T(8,128)(2,1)S(1)}, u32[]{:S(2)}, u32[]{:S(2)}) collective-permute-start(bf16[48,2304]{1,0:T(8,128)(2,1)S(1)} %collective-permute-done.24.refs_2_.refs_14_), channel_id=1, source_target_pairs={{0,8},{4,12},{8,0},{12,4},{16,24},{20,28},{24,16},{28,20},{1,9},{5... | collective-permute-start | bytes 663560 | tf_op jit(solution)/shard_map/ppermute | solution.py:195
  96.3 12.7 %collective-permute-start.10 = (bf16[48,2304]{1,0:T(8,128)(2,1)S(1)}, bf16[48,2304]{1,0:T(8,128)(2,1)S(1)}, u32[]{:S(2)}, u32[]{:S(2)}) collective-permute-start(bf16[48,2304]{1,0:T(8,128)(2,1)S(1)} %collective-permute-done.9.refs_2_.refs_10_), channel_id=1, source_target_pairs={{0,8},{4,12},{8,0},{12,4},{16,24},{20,28},{24,16},{28,20},{1,9},{5... | collective-permute-start | bytes 663560 | tf_op jit(solution)/shard_map/ppermute | solution.py:195
  114.6 30.5 %collective-permute-start.31 = (bf16[3,256,768]{2,1,0:T(8,128)(2,1)}, bf16[3,256,768]{2,1,0:T(8,128)(2,1)S(1)}, u32[]{:S(2)}, u32[]{:S(2)}) collective-permute-start(bf16[3,256,768]{2,1,0:T(8,128)(2,1)} %get-tuple-element.78), channel_id=1, source_target_pairs={{0,4},{4,0},{8,12},{12,8},{16,20},{20,16},{24,28},{28,24},{1,5},{5... | collective-permute-start | bytes 3538952 | tf_op jit(solution)/shard_map/ppermute | solution.py:195
  118.8 8.1 %collective-permute-start.26 = (bf16[2,48,512]{2,1,0:T(8,128)(2,1)}, bf16[2,48,512]{2,1,0:T(8,128)(2,1)}, u32[]{:S(2)}, u32[]{:S(2)}) collective-permute-start(bf16[2,48,512]{2,1,0:T(8,128)(2,1)} %get-tuple-element.70), channel_id=1, source_target_pairs={{0,8},{4,12},{8,0},{12,4},{16,24},{20,28},{24,16},{28,20},{1,9},{5... | collective-permute-start | bytes 294920 | tf_op jit(solution)/shard_map/ppermute | solution.py:195
  118.8 10.6 %collective-permute-start.27 = (bf16[2,48,512]{2,1,0:T(8,128)(2,1)}, bf16[2,48,512]{2,1,0:T(8,128)(2,1)}, u32[]{:S(2)}, u32[]{:S(2)}) collective-permute-start(bf16[2,48,512]{2,1,0:T(8,128)(2,1)} %get-tuple-element.71), channel_id=1, source_target_pairs={{0,16},{4,20},{8,24},{12,28},{16,0},{20,4},{24,8},{28,12},{1,17},{... | collective-permute-start | bytes 294920 | tf_op jit(solution)/shard_map/ppermute | solution.py:195
  121.3 9.9 %collective-permute-start.28 = (bf16[2,48,512]{2,1,0:T(8,128)(2,1)}, bf16[2,48,512]{2,1,0:T(8,128)(2,1)}, u32[]{:S(2)}, u32[]{:S(2)}) collective-permute-start(bf16[2,48,512]{2,1,0:T(8,128)(2,1)} %get-tuple-element.72), channel_id=1, source_target_pairs={{0,24},{4,28},{8,16},{12,20},{16,8},{20,12},{24,0},{28,4},{1,25},{... | collective-permute-start | bytes 294920 | tf_op jit(solution)/shard_map/ppermute | solution.py:195
  126.8 6.2 %collective-permute-start.11 = (bf16[2,48,512]{2,1,0:T(8,128)(2,1)}, bf16[2,48,512]{2,1,0:T(8,128)(2,1)}, u32[]{:S(2)}, u32[]{:S(2)}) collective-permute-start(bf16[2,48,512]{2,1,0:T(8,128)(2,1)} %get-tuple-element.54), channel_id=1, source_target_pairs={{0,8},{4,12},{8,0},{12,4},{16,24},{20,28},{24,16},{28,20},{1,9},{5... | collective-permute-start | bytes 294920 | tf_op jit(solution)/shard_map/ppermute | solution.py:195
  126.8 6.3 %collective-permute-start.12 = (bf16[2,48,512]{2,1,0:T(8,128)(2,1)}, bf16[2,48,512]{2,1,0:T(8,128)(2,1)}, u32[]{:S(2)}, u32[]{:S(2)}) collective-permute-start(bf16[2,48,512]{2,1,0:T(8,128)(2,1)} %get-tuple-element.55), channel_id=1, source_target_pairs={{0,16},{4,20},{8,24},{12,28},{16,0},{20,4},{24,8},{28,12},{1,17},{... | collective-permute-start | bytes 294920 | tf_op jit(solution)/shard_map/ppermute | solution.py:195
  129.4 6.8 %collective-permute-start.13 = (bf16[2,48,512]{2,1,0:T(8,128)(2,1)}, bf16[2,48,512]{2,1,0:T(8,128)(2,1)}, u32[]{:S(2)}, u32[]{:S(2)}) collective-permute-start(bf16[2,48,512]{2,1,0:T(8,128)(2,1)} %get-tuple-element.56), channel_id=1, source_target_pairs={{0,24},{4,28},{8,16},{12,20},{16,8},{20,12},{24,0},{28,4},{1,25},{... | collective-permute-start | bytes 294920 | tf_op jit(solution)/shard_map/ppermute | solution.py:195
  133.0 7.6 %collective-permute-start.29 = (bf16[4,2,24,512]{3,2,1,0:T(8,128)(2,1)}, bf16[4,2,24,512]{3,2,1,0:T(8,128)(2,1)}, u32[]{:S(2)}, u32[]{:S(2)}) collective-permute-start(bf16[4,2,24,512]{3,2,1,0:T(8,128)(2,1)} %get-tuple-element.73), channel_id=1, source_target_pairs={{0,2},{1,3},{2,0},{3,1},{4,6},{5,7},{6,4},{7,5},{8,10},{9,11},{10,... | collective-permute-start | bytes 589832 | tf_op jit(solution)/shard_map/ppermute | solution.py:201
  133.0 7.7 %collective-permute-start.30 = (bf16[4,2,24,512]{3,2,1,0:T(8,128)(2,1)}, bf16[4,2,24,512]{3,2,1,0:T(8,128)(2,1)}, u32[]{:S(2)}, u32[]{:S(2)}) collective-permute-start(bf16[4,2,24,512]{3,2,1,0:T(8,128)(2,1)} %get-tuple-element.74), channel_id=1, source_target_pairs={{0,3},{1,2},{2,1},{3,0},{4,7},{5,6},{6,5},{7,4},{8,11},{9,10},{10,... | collective-permute-start | bytes 589832 | tf_op jit(solution)/shard_map/ppermute | solution.py:201
  138.0 2.7 %collective-permute-start.14 = (bf16[4,2,24,512]{3,2,1,0:T(8,128)(2,1)}, bf16[4,2,24,512]{3,2,1,0:T(8,128)(2,1)}, u32[]{:S(2)}, u32[]{:S(2)}) collective-permute-start(bf16[4,2,24,512]{3,2,1,0:T(8,128)(2,1)} %get-tuple-element.58), channel_id=1, source_target_pairs={{0,1},{1,0},{2,3},{3,2},{4,5},{5,4},{6,7},{7,6},{8,9},{9,8},{10,11... | collective-permute-start | bytes 589832 | tf_op jit(solution)/shard_map/ppermute | solution.py:201
  (24 other events, 109.3 us)
